TPU v7x, 128 devices: a whole 4x4x4 slice. The times are simulated.
128 devices in a mesh: tm: 16 (over z_lo, y, core), head: 8 (over z_hi, x).
Axes of the slice: x: 4, y: 4, z: 4 (z_hi: 2, z_lo: 2; z = z_hi * 2 + z_lo), core: 2. Of those that a mesh axis runs over, the one named last changes fastest.
Arguments:
- query_vectors: bfloat16 [16384, 4096], P('tm', 'head'), may hold values from -6 to 6
- key_vectors: bfloat16 [16384, 4096], P('tm', 'head'), may hold values from -0.125 to 0.125
- value_vectors: bfloat16 [16384, 4096], P('tm', 'head'), may hold values from -6 to 6
- grad_out: bfloat16 [16384, 4096], P('tm', 'head'), may hold values from -8 to 8
- out_weight: bfloat16 [4096, 4096], P('tm', 'head'), may hold values from -0.09375 to 0.09375
- periods: int32 [32], P('head'), may hold values from 1 to 128, as said below
- log_decay: float32 [32, 16384], P('head', 'tm'), may hold values from -0.1109375 to 0, as said below
Outputs:
- query_gradient: bfloat16 [16384, 4096], P('tm', 'head')
- key_gradient: bfloat16 [16384, 4096], P('tm', 'head')
- value_gradient: bfloat16 [16384, 4096], P('tm', 'head')
- grad_weight: float32 [4096, 4096], P('tm', 'head')
Inputs may be any that keep to these rules, and one draw needn't show every extreme that they name: `periods`: some head has period 1 and some head period 128. `log_decay`: Negative.
All inputs are finite; a program needn't handle non-finite values.
Results may differ from a plain program's by a relative error of at most 0.023.
Values may be sent and summed in bfloat16 or wider, within the bound.
A program may use at most 128 MiB of HBM per device.

v0:
```python
import jax
import jax.numpy as jnp
from jax import lax
from jax.sharding import PartitionSpec as P

DK = 128
BLK = 512


def prefix(value, axis, combine, identity, reverse):
    count, place = (lax.axis_size(axis), lax.axis_index(axis))
    everything = jax.tree.map(
        lambda part, kind: lax.all_gather(part.astype(kind), axis),
        value,
        (jnp.bfloat16, jnp.bfloat16),
    )
    start = jax.tree.map(
        lambda part, zero: jnp.broadcast_to(jnp.asarray(zero, part.dtype), part.shape),
        value,
        identity,
    )

    def turn(k, before):
        at = count - 1 - k if reverse else k
        reached = at > place if reverse else at < place
        new = combine(
            before, jax.tree.map(lambda part, own: part[at].astype(own.dtype), everything, value)
        )
        return jax.tree.map(lambda a, b: jnp.where(reached, a, b), new, before)

    return lax.fori_loop(0, count, turn, start)


def block_mask(cumul, update):
    span_len = cumul.shape[1]
    causal = jnp.arange(span_len)[:, None] >= jnp.arange(span_len)[None, :]
    spread = jnp.where(causal[None], cumul[:, :, None] - cumul[:, None, :], -jnp.inf)
    return jnp.exp(spread) * update[:, None, :]


def pair_weights(query_matrix, key_matrix, value_matrix, gradient_rows, cumul, update_rows):
    decay_mask = block_mask(cumul, update_rows)
    scores = jnp.einsum(
        "thk,shk->hts", query_matrix, key_matrix, preferred_element_type=jnp.float32
    )
    reversed_blocks = jnp.einsum(
        "thv,shv->hts", gradient_rows, value_matrix, preferred_element_type=jnp.float32
    )
    return (
        (scores * decay_mask).astype(jnp.bfloat16),
        (reversed_blocks * decay_mask).astype(jnp.bfloat16),
    )


def layer_output(query_matrix, value_matrix, projection_weight, cumul, state_start):
    within = jnp.einsum(
        "hts,shv->thv", projection_weight, value_matrix, preferred_element_type=jnp.float32
    )
    carried_state = jnp.einsum(
        "qml,mla->qma",
        query_matrix,
        state_start.astype(jnp.bfloat16),
        preferred_element_type=jnp.float32,
    )
    return (within + jnp.exp(cumul).T[:, :, None] * carried_state).astype(jnp.bfloat16)


def input_grads(
    query_matrix,
    key_matrix,
    value_matrix,
    gradient_rows,
    projection_weight,
    reversed_blocks,
    cumul,
    update_rows,
    state_start,
    finish,
):
    state_reduced = state_start.astype(jnp.bfloat16)
    carry_reduced = finish.astype(jnp.bfloat16)
    incoming_gradient = jnp.exp(cumul).T[:, :, None]
    outgoing_gradient = (update_rows * jnp.exp(cumul[:, -1][:, None] - cumul)).T[:, :, None]
    query_gradient = jnp.einsum(
        "gea,agq->egq", reversed_blocks, key_matrix, preferred_element_type=jnp.float32
    ) + incoming_gradient * jnp.einsum(
        "sba,bda->sbd", gradient_rows, state_reduced, preferred_element_type=jnp.float32
    )
    key_gradient = jnp.einsum(
        "rwy,wre->yre", reversed_blocks, query_matrix, preferred_element_type=jnp.float32
    ) + outgoing_gradient * jnp.einsum(
        "wqx,qgx->wqg", value_matrix, carry_reduced, preferred_element_type=jnp.float32
    )
    value_gradient = jnp.einsum(
        "kyp,ykb->pkb", projection_weight, gradient_rows, preferred_element_type=jnp.float32
    ) + outgoing_gradient * jnp.einsum(
        "imx,mxd->imd", key_matrix, carry_reduced, preferred_element_type=jnp.float32
    )
    return (
        query_gradient.astype(jnp.bfloat16),
        key_gradient.astype(jnp.bfloat16),
        value_gradient.astype(jnp.bfloat16),
    )


def combine_carry(earlier, later):
    return (earlier[0] * later[0], later[0][:, None, None] * earlier[1] + later[1])


def per_device(query_vectors, key_vectors, value_vectors, grad_out, out_weight, periods, log_decay):
    tok_rows = query_vectors.shape[0]
    head_count = periods.shape[0]
    block_count = tok_rows // BLK
    full_grad = lax.all_gather(grad_out, "head", axis=1, tiled=True)
    columns = full_grad
    grad_mixed = jnp.dot(
        columns,
        lax.all_gather(out_weight, "tm", axis=0, tiled=True),
        preferred_element_type=jnp.float32,
    ).astype(jnp.bfloat16)
    offset = lax.axis_index("tm") * tok_rows
    positions = offset + jnp.arange(tok_rows, dtype=jnp.int32)
    update = (positions[None, :] % periods[:, None] == 0).astype(jnp.float32)
    step_log = update * periods[:, None].astype(jnp.float32) * log_decay
    cumulative = jnp.cumsum(step_log.reshape(head_count, block_count, BLK), axis=2).transpose(
        1, 0, 2
    )
    updates = update.reshape(head_count, block_count, BLK).transpose(1, 0, 2)

    def blocked(tensor):
        return tensor.reshape(block_count, BLK, head_count, DK)

    query_blocks = blocked(query_vectors)
    key_blocks = blocked(key_vectors)
    value_blocks = blocked(value_vectors)
    grad_blocks = blocked(grad_mixed)
    zero_state = jnp.zeros((head_count, DK, DK), jnp.float32)

    def forward(running, section):
        key_matrix, value_matrix, cumul, update_rows = section
        block_total = cumul[:, -1]
        factor = update_rows * jnp.exp(block_total[:, None] - cumul)
        decay_scaled = (key_matrix.astype(jnp.float32) * factor.T[:, :, None]).astype(jnp.bfloat16)
        outer_product = jnp.einsum(
            "ptz,ptb->tzb", decay_scaled, value_matrix, preferred_element_type=jnp.float32
        )
        return (jnp.exp(block_total)[:, None, None] * running + outer_product, running)

    state_local, state_starts = lax.scan(
        forward, zero_state, (key_blocks, value_blocks, cumulative, updates)
    )

    def backward(carried_in, section):
        query_matrix, gradient_rows, cumul = section
        decay_scaled = (query_matrix.astype(jnp.float32) * jnp.exp(cumul).T[:, :, None]).astype(
            jnp.bfloat16
        )
        outer_product = jnp.einsum(
            "yop,yoj->opj", decay_scaled, gradient_rows, preferred_element_type=jnp.float32
        )
        return (jnp.exp(cumul[:, -1])[:, None, None] * carried_in + outer_product, carried_in)

    grad_local, grad_ends = lax.scan(
        backward, zero_state, (query_blocks, grad_blocks, cumulative), reverse=True
    )
    totals = cumulative[:, :, -1]
    shrink = jnp.exp(jnp.sum(totals, axis=0))
    identity = (jnp.ones((head_count,), jnp.float32), zero_state)
    _, state_in = prefix((shrink, state_local), "tm", combine_carry, identity, False)
    _, grad_in = prefix((shrink, grad_local), "tm", combine_carry, identity, True)
    running_sum = jnp.cumsum(totals, axis=0)
    before = running_sum - totals
    later_sum = jnp.sum(totals, axis=0)[None] - running_sum
    starts = jnp.exp(before)[:, :, None, None] * state_in[None] + state_starts
    finishes = jnp.exp(later_sum)[:, :, None, None] * grad_in[None] + grad_ends
    sections = (
        query_blocks,
        key_blocks,
        value_blocks,
        grad_blocks,
        cumulative,
        updates,
        starts,
        finishes,
    )

    def forward_output(section):
        query_matrix, key_matrix, value_matrix, gradient_rows, cumul, update_rows, state_start = (
            section
        )
        projection_weight, reversed_blocks = pair_weights(
            query_matrix, key_matrix, value_matrix, gradient_rows, cumul, update_rows
        )
        return (
            layer_output(query_matrix, value_matrix, projection_weight, cumul, state_start),
            projection_weight,
            reversed_blocks,
        )

    mixed, weight_blocks, backed_blocks = lax.map(forward_output, sections[:7])
    mixed_rows = mixed.reshape(tok_rows, head_count * DK)
    columns = full_grad
    grad_weight = lax.psum_scatter(
        lax.dot_general(
            columns, mixed_rows, (((0,), (0,)), ((), ())), preferred_element_type=jnp.float32
        ).astype(jnp.bfloat16),
        "tm",
        scatter_dimension=0,
        tiled=True,
    ).astype(jnp.float32)

    def gradient_output(section):
        (
            query_matrix,
            key_matrix,
            value_matrix,
            gradient_rows,
            cumul,
            update_rows,
            state_start,
            finish,
            projection_weight,
            reversed_blocks,
        ) = section
        return input_grads(
            query_matrix,
            key_matrix,
            value_matrix,
            gradient_rows,
            projection_weight,
            reversed_blocks,
            cumul,
            update_rows,
            state_start,
            finish,
        )

    query_gradient, key_gradient, value_gradient = lax.map(
        gradient_output, sections + (weight_blocks, backed_blocks)
    )
    return (
        query_gradient.reshape(tok_rows, head_count * DK),
        key_gradient.reshape(tok_rows, head_count * DK),
        value_gradient.reshape(tok_rows, head_count * DK),
        grad_weight,
    )


def solution(mesh):
    return jax.shard_map(
        per_device,
        mesh=mesh,
        in_specs=(
            P("tm", "head"),
            P("tm", "head"),
            P("tm", "head"),
            P("tm", "head"),
            P("tm", "head"),
            P("head"),
            P("head", "tm"),
        ),
        out_specs=(P("tm", "head"), P("tm", "head"), P("tm", "head"), P("tm", "head")),
        check_vma=False,
    )
```

profile of v0, /device:TPU:1, one launch (start us, length us, event | category | flops | bytes accessed | tf_op | source)
XLA Modules:
  0.0 382.9 jit_solution(7410916782412862764)
XLA Ops:
  11.3 2.4 reduce-window.6
  21.0 5.9 %fusion.90 = f32[2,4,512]{1,2,0:T(8,128)} fusion(s32[4]{0:T(128)S(1)} %get-tuple-element.848, s32[2,512]{1,0:T(2,128)S(1)} %add_add_fusion, pred[4]{0:T(512)(128)(4,1)S(1)} %broadcast_compare_fusion), kind=kLoop, calls=%fused_computation.136 | loop fusion | flops 36864 | bytes 20500 | tf_op jit(solution)/shard_map/convert_element_type | solution.py:123
  27.8 4.4 %while.90 = (s32[]{:T(128)}, f32[4,128,128]{2,1,0:T(8,128)S(1)}, f32[2,4,128,128]{3,2,1,0:T(8,128)}, f32[2,4,512]{1,2,0:T(8,128)S(1)}, bf16[2,512,4,128]{1,3,2,0...) while((s32[]{:T(128)}, f32[4,128,128]{2,1,0:T(8,128)S(1)}, ...), condition=%wide.region_5.6_spmd.clone, body=%wide.region_4.5_spmd.clone.sunk | while | flops 68161536 | bytes 2164928 | solution.py:149
  37.2 28.8 %all-reduce = bf16[64]{0:T(256)(128)(2,1)S(1)} all-reduce(bf16[64]{0:T(256)(128)(2,1)S(1)} %dynamic-update-slice), channel_id=2, replica_groups=mesh['tm'=16,'head'=8] {'tm'}, use_global_device_ids=true, to_apply=%add | all-reduce | flops 64 | bytes 256
  68.3 2.4 copy.84
  70.8 99.7 %all-gather.8.cloned.1.call-done = bf16[1024,4096]{1,0:T(8,128)(2,1)} async-done(((bf16[1024,512]{1,0:T(8,128)(2,1)}), bf16[1024,4096]{1,0:T(8,128)(2,1)}) %all-gather.8.cloned.1.call-update) | async-done | bytes 8388624 | tf_op jit(solution)/shard_map/all_gather | solution.py:114
  170.6 10.0 %convolution_convert_fusion.1 = bf16[1024,512]{1,0:T(8,128)(2,1)} fusion(bf16[1024,4096]{1,0:T(8,128)(2,1)} %all-gather.8.cloned.1.call-done, bf16[4096,512]{1,0:T(8,128)(2,1)} %all-gather.10.cloned.1.call-done), kind=kOutput, calls=%fused_computation.123 | convolution fusion | flops 4295491584 | bytes 13631488 | tf_op jit(solution)/shard_map/dot_general | solution.py:116
  185.0 7.2 %while.92 = (s32[]{:T(128)}, f32[4,128,128]{2,1,0:T(8,128)S(1)}, f32[2,4,128,128]{3,2,1,0:T(8,128)}, f32[2,4,512]{1,2,0:T(8,128)S(1)}, bf16[2,512,4,128]{1,3,2,0...) while((s32[]{:T(128)}, f32[4,128,128]{2,1,0:T(8,128)S(1)}, ...), condition=%wide.region_9.10_spmd.clone, body=%wide.region_8.9_spmd.clone.sunk | while | flops 68157440 | bytes 2148499 | solution.py:163
  193.0 13.4 %all-gather.12.cloned.1.call-done = bf16[64,128,128]{2,1,0:T(8,128)(2,1)} async-done(((bf16[4,128,128]{2,1,0:T(8,128)(2,1)}), bf16[64,128,128]{2,1,0:T(8,128)(2,1)}) %all-gather.12.cloned.1.call-update) | async-done | bytes 2097168 | tf_op jit(solution)/shard_map/all_gather | solution.py:13
  206.4 28.6 %while.91 = (s32[]{:T(128)}, f32[4,128,128]{2,1,0:T(8,128)}, s32[]{:T(128)}, bf16[16,4]{1,0:T(8,128)(2,1)S(1)}, bf16[16,4,128,128]{3,2,1,0:T(8,128)(2,1)}, /*index=5*/s32[]{:T(128)}, s32[]{:T(128)}) while((s32[]{:T(128)}, f32[4,128,128]{2,1,0:T(8,128)}, s32[]{:T(128)}, bf16[16,4]{1,0:T(8,128)(2,1)S(1)}, ...), condition=%wide.region_7.8_spmd.clone, body=%wide.region_6.7_spmd.clone.sunk | while | flops 327688 | bytes 655505 | solution.py:31
  235.0 7.0 %all-gather.14.cloned.1.call-done = bf16[64,128,128]{2,1,0:T(8,128)(2,1)} async-done(((bf16[4,128,128]{2,1,0:T(8,128)(2,1)}), bf16[64,128,128]{2,1,0:T(8,128)(2,1)}) %all-gather.14.cloned.1.call-update) | async-done | bytes 2097168 | tf_op jit(solution)/shard_map/all_gather | solution.py:13
  242.0 17.0 %while.93 = (s32[]{:T(128)}, f32[4,128,128]{2,1,0:T(8,128)S(1)}, s32[]{:T(128)}, bf16[16,4]{1,0:T(8,128)(2,1)S(1)}, bf16[16,4,128,128]{3,2,1,0:T(8,128)(2,1)}, /*index=5*/s32[]{:T(128)}, s32[]{:T(128)}, s32[]{:T(128)}, s32[]{:T(128)}) while((s32[]{:T(128)}, f32[4,128,128]{2,1,0:T(8,128)S(1)}, s32[]{:T(128)}, ...), condition=%wide.region_11.12_spmd.clone, body=%wide.region_10.11_spmd.clone.sunk | while | flops 327692 | bytes 655567 | solution.py:31
  262.4 38.4 %while.88 = (s32[]{:T(128)}, bf16[2,512,4,128]{3,2,1,0:T(4,128)(2,1)}, bf16[2,4,512,512]{3,2,1,0:T(8,128)(2,1)}, bf16[2,4,512,512]{3,2,1,0:T(8,128)(2,1)}, bf16[...) while((s32[]{:T(128)}, ...), condition=%wide.region_13.14_spmd, body=%wide.region_12.13_spmd.sunk | while | flops 883949568 | bytes 30411028 | solution.py:200
  265.5 2.9 bitcast_dynamic-update-slice_fusion.8
  269.8 2.6 convolution_bitcast_fusion.6
  278.0 3.6 bitcast_dynamic-update-slice_fusion.9
  284.7 2.9 bitcast_dynamic-update-slice_fusion.8
  289.0 2.6 convolution_bitcast_fusion.6
  297.2 3.6 bitcast_dynamic-update-slice_fusion.9
  300.8 10.2 %fusion.86 = bf16[4096,512]{0,1:T(8,128)(2,1)} fusion(bf16[1024,4096]{1,0:T(8,128)(2,1)} %all-gather.8.cloned.1.call-done, bf16[128,8,4,128]{3,2,1,0:T(4,128)(2,1)} %bitcast.351), kind=kOutput, calls=%fused_computation.122 | convolution fusion | flops 4297064448 | bytes 13631488 | tf_op jit(solution)/shard_map/dot_general | solution.py:204
  314.8 39.6 %while.89 = (s32[]{:T(128)}, bf16[2,512,4,128]{3,2,1,0:T(4,128)(2,1)}, bf16[2,512,4,128]{3,2,1,0:T(4,128)(2,1)}, bf16[2,512,4,128]{3,2,1,0:T(4,128)(2,1)}, bf16[...) while((s32[]{:T(128)}, ...), condition=%wide.region_15.16_spmd, body=%wide.region_14.15_spmd.sunk | while | flops 1008996352 | bytes 24100036 | solution.py:238
  341.5 2.4 fusion.156
  354.4 2.5 copy.128
  360.4 14.0 %reduce-scatter.2.cloned.1.call-done = bf16[256,512]{0,1:T(8,128)(2,1)} async-done(((bf16[4096,512]{0,1:T(8,128)(2,1)}), bf16[256,512]{0,1:T(8,128)(2,1)}) %reduce-scatter.2.cloned.1.call-update) | async-done | bytes 262160 | tf_op jit(solution)/shard_map/reduce_scatter | solution.py:203
  (229 shorter events, 150.1 us)
Async XLA Ops:
  7.2 63.7 %all-gather.10.cloned.1.call-start = ((), (), s32[]{:S(2)}) async-start(), calls=%async_computation.2 | async-start | bytes 4456448 | tf_op jit(solution)/shard_map/all_gather | solution.py:118
  7.9 162.7 %all-gather.8.cloned.1.call-start = ((), (), s32[]{:S(2)}) async-start(), calls=%async_computation.1 | async-start | bytes 9437184 | tf_op jit(solution)/shard_map/all_gather | solution.py:114
  8.6 197.7 %all-gather.12.cloned.1.call-start = ((), (), s32[]{:S(2)}) async-start(), calls=%async_computation.4 | async-start | bytes 2228224 | tf_op jit(solution)/shard_map/all_gather | solution.py:13
  16.3 1.0 copy-start.3
  27.8 7.9 %copy-start.10 = (u32[128]{0:T(128)S(1)}, u32[128]{0:T(128)}, u32[]{:S(2)}) copy-start(u32[128]{0:T(128)} %constant.190) | copy-start | bytes 1540
  32.2 148.4 %copy-start.2 = (bf16[2,512,4,128]{3,1,2,0:T(8,128)(2,1)}, bf16[2,512,4,128]{3,1,2,0:T(8,128)(2,1)S(1)}, u32[]{:S(2)}) copy-start(bf16[2,512,4,128]{3,1,2,0:T(8,128)(2,1)S(1)} %get-tuple-element.1360) | copy-start | bytes 3145732
  33.0 209.0 %all-gather.14.cloned.1.call-start = ((), (), s32[]{:S(2)}) async-start(), calls=%async_computation.5 | async-start | bytes 2228224 | tf_op jit(solution)/shard_map/all_gather | solution.py:13
  192.2 68.9 %copy-start = (f32[2,4,512]{1,2,0:T(8,128)}, f32[2,4,512]{1,2,0:T(8,128)S(1)}, u32[]{:S(2)}) copy-start(f32[2,4,512]{1,2,0:T(8,128)S(1)} %get-tuple-element.1359) | copy-start | bytes 49156
  192.9 66.1 %copy-start.8 = (f32[2,4,128,128]{3,2,1,0:T(8,128)S(1)}, f32[2,4,128,128]{3,2,1,0:T(8,128)}, u32[]{:S(2)}) copy-start(f32[2,4,128,128]{3,2,1,0:T(8,128)} %get-tuple-element.530) | copy-start | bytes 1572868
  192.9 181.5 %reduce-scatter.2.cloned.1.call-start = ((), (), s32[]{:S(2)}) async-start(), calls=%async_computation.3 | async-start | bytes 4456448 | tf_op jit(solution)/shard_map/reduce_scatter | solution.py:203
  263.9 1.6 copy-start.1
  265.4 3.0 copy-start.9
  265.5 3.0 copy-start.5
  265.5 2.9 copy-start.4
  273.4 4.6 %copy-start.6 = (pred[512,512]{1,0:T(8,128)(4,1)S(1)}, pred[512,512]{1,0:T(8,128)(4,1)}, u32[]{:S(2)}) copy-start(pred[512,512]{1,0:T(8,128)(4,1)} %copy-done.5) | copy-start | bytes 786436 | tf_op jit(solution)/shard_map/while
  283.1 1.6 copy-start.1
  284.6 3.0 copy-start.9
  284.7 3.0 copy-start.5
  284.7 2.9 copy-start.4
  292.6 4.6 %copy-start.6 = (pred[512,512]{1,0:T(8,128)(4,1)S(1)}, pred[512,512]{1,0:T(8,128)(4,1)}, u32[]{:S(2)}) copy-start(pred[512,512]{1,0:T(8,128)(4,1)} %copy-done.5) | copy-start | bytes 786436 | tf_op jit(solution)/shard_map/while
  354.4 4.9 %copy-start.7 = (bf16[2,512,4,128]{3,2,1,0:T(4,128)(2,1)S(1)}, bf16[2,512,4,128]{3,2,1,0:T(4,128)(2,1)}, u32[]{:S(2)}) copy-start(bf16[2,512,4,128]{3,2,1,0:T(4,128)(2,1)} %get-tuple-element.532) | copy-start | bytes 3145732
Sparse Core Ops, SparseCore 0:
  9.7 40.8 all-gather.9
  52.8 117.7 all-gather.7
  172.3 34.0 all-gather.11
  207.9 33.9 all-gather.13
  311.2 63.2 reduce-scatter.1
where the time goes:
time: 389 us; the launch traced here: 383 us
  waiting for transfers between devices  136 us (35%)
  matrix products  69 us (18%)
  other arithmetic  67.4 us (17%)
  local copies, waits for them, and re-layouts  66.2 us (17%)
  blocking collectives  28.8 us (7%)
  between operations  14.6 us (4%)
    all_gather x1, waiting for transfers between devices, per_device(): full_grad = lax.all_gather(grad_out, 'head', axis=1, tiled=True)  99.7 us
    select_n x32, other arithmetic, turn(): return jax.tree.map(lambda a, b: jnp.where(reached, a, b), new, before)  44.7 us
    unnamed x1, blocking collectives  28.8 us
    all_gather x2, waiting for transfers between devices, prefix(): lax.all_gather(part.astype(kind), axis)  20.4 us
    dynamic_update_slice x14, local copies, waits for them, and re-layouts, per_device(): mixed, weight_blocks, backed_blocks = lax.map(forward_output, sections[:7])  16.8 us
    reduce_scatter x1, waiting for transfers between devices, per_device(): lax.psum_scatter(lax.dot_general(columns, mixed_rows, (((0,), (0,)), ((),...  14 us
    dot_general x1, matrix products, per_device(): lax.dot_general(columns, mixed_rows, (((0,), (0,)), ((), ())), preferred_...  10.2 us
    dot_general x1, matrix products, per_device(): jnp.dot(columns, lax.all_gather(out_weight, 'tm', axis=0, tiled=True), pr...  10 us
  transfers between devices with their start and end apart: 5, of which 4 were waited for; matrix products, arithmetic and copies ran while one was open for 34% of the time, Pallas kernels for 0%

commit v1 on v0

v1 whole, which is shorter than its diff:
```python
import jax
import jax.numpy as jnp
from jax import lax
from jax.experimental import pallas as pl
from jax.experimental.pallas import tpu as pltpu
from jax.sharding import PartitionSpec as P

DK = 128
BLK = 512
NH = 4
TM = 16
ROWS = 1024
HALF = 256
BF = jnp.bfloat16
F32 = jnp.float32
MESH = pl.DeviceIdType.MESH


def mm(a, b):
    return jnp.dot(a, b, preferred_element_type=F32)


def mm_nt(a, b):
    return lax.dot_general(a, b, (((1,), (1,)), ((), ())), preferred_element_type=F32)


def mm_tn(a, b):
    return lax.dot_general(a, b, (((0,), (0,)), ((), ())), preferred_element_type=F32)


def column(row):
    return jnp.transpose(jnp.broadcast_to(row, (DK, row.shape[1])))


def kernel(
    per_ref,
    ld_ref,
    q_hbm,
    k_hbm,
    v_hbm,
    g_hbm,
    w_hbm,
    dq_ref,
    dk_ref,
    dv_ref,
    gw_ref,
    q,
    k,
    v,
    e,
    grads,
    weight,
    acc,
    cum,
    upd,
    fcol,
    ecol,
    mask,
    wts,
    qst,
    mixt,
    st,
    sb,
    rl,
    dvp,
    tx_s,
    rx_s,
    tx_p,
    rx_p,
    tx_r,
    rx_r,
    tx_o,
    rx_o,
    dec,
    pair_tx,
    pair_rx,
    pair_own,
    y_tx,
    y_rx,
    z_tx,
    z_rx,
    load_sem,
    ag_send,
    ag_recv,
    w_send,
    w_recv,
    s_send,
    s_recv,
    c_send,
    c_recv,
    y_send,
    y_recv,
    z_send,
    z_recv,
):
    tm = lax.axis_index("tm")
    hd = lax.axis_index("head")
    x = lax.rem(hd, 4)
    zh = hd // 4
    right = zh * 4 + lax.rem(x + 1, 4)
    left = zh * 4 + lax.rem(x + 3, 4)
    far = zh * 4 + lax.rem(x + 2, 4)
    across = lax.rem(hd + 4, 8)
    core = lax.rem(tm, 2)
    y = lax.rem(tm // 2, 4)
    zl = tm // 8
    mate = tm + 1 - 2 * core

    def tm_at(zl_, y_, core_):
        return (zl_ * 4 + y_) * 2 + core_

    def local(src, dst, i):
        return pltpu.make_async_copy(src, dst, load_sem.at[i])

    loads = [
        local(q_hbm, q, 0),
        local(k_hbm, k, 1),
        local(v_hbm, v, 2),
        local(g_hbm, grads.at[hd], 3),
        local(w_hbm, weight.at[tm // 2, pl.ds(core * HALF, HALF)], 4),
    ]
    for item in loads:
        item.start()

    barrier = pltpu.get_barrier_semaphore()
    for d in range(1, TM):
        pl.semaphore_signal(
            barrier, inc=1, device_id={"tm": lax.rem(tm + d, TM)}, device_id_type=MESH
        )
    for peer in (right, left, across):
        pl.semaphore_signal(barrier, inc=1, device_id={"head": peer}, device_id_type=MESH)
    pl.semaphore_wait(barrier, TM + 2)

    sent = []

    def send(src, dst, send_sem, recv_sem, device):
        copy = pltpu.make_async_remote_copy(
            src_ref=src,
            dst_ref=dst,
            send_sem=send_sem,
            recv_sem=recv_sem,
            device_id=device,
            device_id_type=MESH,
        )
        copy.start()
        sent.append(copy)
        return copy

    def gather(src, slot, first, count, peer, n):
        rows = pl.ds(first, count)
        return send(
            src.at[rows],
            grads.at[slot, rows],
            ag_send.at[n],
            ag_recv.at[n],
            {"head": peer},
        )

    to_right = [gather(g_hbm, hd, c * 512, 512, right, c) for c in range(2)]
    to_left = [gather(g_hbm, hd, c * 512, 512, left, 2 + c) for c in range(2)]
    to_across = [gather(g_hbm, hd, 0, 512, across, 4)]

    def w_copy(src, owner, device, n):
        return send(
            src,
            weight.at[owner // 2, pl.ds(lax.rem(owner, 2) * HALF, HALF)],
            w_send.at[n],
            w_recv.at[n],
            {"tm": device},
        )

    def w_block(owner):
        return weight.at[owner // 2, pl.ds(lax.rem(owner, 2) * HALF, HALF)]

    ids = lax.broadcasted_iota(jnp.int32, (8, BLK), 0)
    lane = lax.broadcasted_iota(jnp.int32, (8, BLK), 1)
    head_of = lax.rem(ids, NH)
    period = jnp.full((8, BLK), per_ref[0], jnp.int32)
    for h in range(1, NH):
        period = jnp.where(head_of == h, per_ref[h], period)
    period = period.astype(F32)
    pos = (tm * ROWS + (ids // NH) * BLK + lane).astype(F32)
    turns = jnp.floor((pos + 0.5) * (1.0 / period))
    update = jnp.where(pos == turns * period, 1.0, 0.0).astype(F32)
    cum[0:NH, :] = ld_ref[:, 0:BLK]
    cum[NH : 2 * NH, :] = ld_ref[:, BLK : 2 * BLK]
    run = update * period * cum[...]
    shift = 1
    while shift < BLK:
        run = run + jnp.where(lane >= shift, pltpu.roll(run, shift, axis=1), 0.0)
        shift *= 2
    cum[...] = run
    upd[...] = update

    def rows_of(p):
        return cum[pl.ds(p, 1), :], upd[pl.ds(p, 1), :]

    def total_of(p):
        row = cum[pl.ds(p, 1), :]
        return jnp.broadcast_to(row[:, BLK - 1 : BLK], (1, DK))

    def cols(h):
        return pl.ds(pl.multiple_of(h * DK, DK), DK)

    for i in range(3):
        loads[i].wait()

    @pl.loop(0, NH)
    def _(h):
        for b in range(2):
            p = b * NH + h
            row, urow = rows_of(p)
            factor = column(urow * jnp.exp(row[:, BLK - 1 : BLK] - row))
            fcol[p] = factor
            scaled = (k[b * BLK : (b + 1) * BLK, cols(h)].astype(F32) * factor).astype(BF)
            st[p] = mm_tn(scaled, v[b * BLK : (b + 1) * BLK, cols(h)])
        t0, t1 = total_of(h), total_of(NH + h)
        whole = jnp.exp(t1) * st[h] + st[NH + h]
        for u in range(4):
            tx_s[h * 4 + u, 0:32] = whole[32 * u : 32 * u + 32]
            tx_s[h * 4 + u, 32:40] = jnp.broadcast_to(t0 + t1, (8, DK))

    def exchange(tx, rx, kind):
        copies = []
        for d in range(1, TM):
            peer = lax.rem(tm + d, TM)
            n = kind * TM + d
            copies.append(
                send(tx.at[peer], rx.at[tm], s_send.at[n], s_recv.at[n], {"tm": peer})
            )
        return copies

    s_first = exchange(tx_s, rx_s, 0)
    rx_s[tm] = tx_s[tm]
    to_across.append(gather(g_hbm, hd, 512, 512, across, 5))
    w_across = w_copy(w_hbm, tm, tm_at(1 - zl, y, core), 0)
    w_near = [
        w_copy(w_hbm, tm, tm_at(zl, lax.rem(y + d, 4), core), d) for d in range(1, 4)
    ]
    w_pair = [w_copy(w_hbm, tm, mate, 7)]

    @pl.loop(0, NH)
    def _(h):
        low = lax.broadcasted_iota(jnp.int32, (HALF, HALF), 0) >= lax.broadcasted_iota(
            jnp.int32, (HALF, HALF), 1
        )
        for b in range(2):
            p = b * NH + h
            row, urow = rows_of(p)
            at = column(row)
            grown = jnp.exp(at)
            ecol[p] = grown
            qb = q[b * BLK : (b + 1) * BLK, cols(h)]
            kb = k[b * BLK : (b + 1) * BLK, cols(h)]
            qst[p] = jnp.transpose(qb.astype(F32) * grown).astype(BF)
            wide = jnp.concatenate([at, at], axis=1)
            for n, (ti, si) in enumerate(((0, 0), (1, 0), (1, 1))):
                gap = wide[ti * HALF : (ti + 1) * HALF] - row[:, si * HALF : (si + 1) * HALF]
                if ti == si:
                    gap = jnp.where(low, gap, -jnp.inf)
                tile = jnp.exp(gap) * urow[:, si * HALF : (si + 1) * HALF]
                mask[p, n] = tile
                score = mm_nt(qb[ti * HALF : (ti + 1) * HALF], kb[si * HALF : (si + 1) * HALF])
                wts[p, n] = (tile * score).astype(BF)

    w_across.wait_recv()
    z_mate = tm_at(1 - zl, y, core)
    w_far = [
        w_copy(w_block(z_mate), z_mate, tm_at(zl, lax.rem(y + d, 4), core), 3 + d)
        for d in range(1, 4)
    ]
    w_pair.append(w_copy(w_block(z_mate), z_mate, mate, 8))
    on_right, on_left = [], []

    def pass_x(c):
        to_right[c].wait_recv()
        on_right.append(gather(grads.at[left], left, c * 512, 256, right, 6 + c))
        to_left[c].wait_recv()
        on_left.append(gather(grads.at[right], right, c * 512 + 256, 256, left, 8 + c))

    pass_x(0)

    for copy in s_first:
        copy.wait_recv()
    part = jnp.zeros((32, DK), F32)
    for i in range(TM):
        tx_p[i] = part.astype(BF)
        fall = jnp.exp(rx_s[i, 32:40])
        dec[i] = fall
        part = jnp.concatenate([fall] * 4, axis=0) * part + rx_s[i, 0:32]
    s_second = exchange(tx_p, rx_p, 1)
    rx_p[tm] = tx_p[tm]

    for d in range(1, 4):
        src = tm_at(zl, lax.rem(y + 4 - d, 4), core)
        w_near[d - 1].wait_recv()
        w_pair.append(w_copy(w_block(src), src, mate, 8 + d))
    pass_x(1)
    p_right, p_left = [], []

    def pass_z(c):
        to_across[c].wait_recv()
        p_right.append(gather(grads.at[across], across, c * 512, 512, right, 10 + c))
        p_left.append(gather(grads.at[across], across, c * 512, 512, left, 12 + c))

    pass_z(0)
    for d in range(1, 4):
        src = tm_at(1 - zl, lax.rem(y + 4 - d, 4), core)
        w_far[d - 1].wait_recv()
        w_pair.append(w_copy(w_block(src), src, mate, 11 + d))

    for copy in s_second:
        copy.wait_recv()

    @pl.loop(0, NH)
    def _(h):
        start = rx_p[pl.ds(h * 4, 4)].reshape(DK, DK).astype(F32)
        starts = (start, jnp.exp(total_of(h)) * start + st[h])
        for b in range(2):
            p = b * NH + h
            state = starts[b].astype(BF)
            sb[p] = state
            rows = slice(b * BLK, (b + 1) * BLK)
            v0 = v[b * BLK : b * BLK + HALF, cols(h)]
            v1 = v[b * BLK + HALF : (b + 1) * BLK, cols(h)]
            within = jnp.concatenate(
                [mm(wts[p, 0], v0), mm(wts[p, 1], v0) + mm(wts[p, 2], v1)], axis=0
            )
            mixed = within + ecol[p] * mm(q[rows, cols(h)], state)
            mixt[cols(h), rows] = jnp.transpose(mixed).astype(BF)

    pass_z(1)
    on_across = []

    def pass_far(c):
        on_right[c].wait_recv()
        on_across.append(gather(grads.at[far], far, c * 512, 256, across, 14 + 2 * c))
        on_left[c].wait_recv()
        on_across.append(gather(grads.at[far], far, c * 512 + 256, 256, across, 15 + 2 * c))

    pass_far(0)

    @pl.loop(0, 4)
    def _(r):
        acc[pl.ds(r * HALF, HALF), :] = jnp.zeros((HALF, NH * DK), F32)

    def grow_mixed(s):
        @pl.loop(0, 4)
        def _(r):
            rows = pl.ds(pl.multiple_of(r * HALF, HALF), HALF)
            acc[rows, :] += mm(grads[s, rows, :], weight[s])

    mine = pl.ds(pl.multiple_of(core * HALF, HALF), HALF)
    other = pl.ds(pl.multiple_of((1 - core) * HALF, HALF), HALF)
    pairs = []

    def grow_weight(s, n):
        @pl.loop(0, 2)
        def _(r):
            rows = pl.ds(pl.multiple_of(r * HALF, HALF), HALF)
            pair_tx[n, rows, :] = mm(mixt[rows, :], grads[s, :, other]).astype(BF)

        pairs.append(
            send(pair_tx.at[n], pair_rx.at[n], c_send.at[n], c_recv.at[n], {"tm": mate})
        )

        @pl.loop(0, 2)
        def _(r):
            rows = pl.ds(pl.multiple_of(r * HALF, HALF), HALF)
            pair_own[n % 4, rows, :] = mm(mixt[rows, :], grads[s, :, mine])

    def y_copy(s, n):
        gap = lax.rem(lax.rem(s, 4) + 4 - y, 4)
        slot = (s // 4) * 4
        return gap, pltpu.make_async_remote_copy(
            src_ref=y_tx.at[n],
            dst_ref=y_rx.at[slot + y],
            send_sem=y_send.at[n],
            recv_sem=y_recv.at[slot + gap],
            device_id={"tm": tm_at(zl, lax.rem(s, 4), core)},
            device_id_type=MESH,
        )

    def add_pair(s, n):
        pairs[n].wait_recv()
        y_tx[n] = (pair_own[n % 4] + pair_rx[n].astype(F32)).astype(BF)
        gap, copy = y_copy(s, n)

        @pl.when(gap != 0)
        def _():
            copy.start()

        @pl.when(gap == 0)
        def _():
            y_rx[(s // 4) * 4 + y] = y_tx[n]

    z_right = lax.rem(right + 4, 8)
    z_left = lax.rem(left + 4, 8)
    z_far = lax.rem(far + 4, 8)
    order = [hd, right, left, across, far, z_far, z_left, z_right]

    loads[3].wait()
    loads[4].wait()
    for copy in w_pair:
        copy.wait_recv()
    grow_weight(order[0], 0)
    grow_mixed(order[0])
    pass_far(1)
    for n in range(1, 4):
        grow_weight(order[n], n)
        add_pair(order[n - 1], n - 1)
        grow_mixed(order[n])
    grow_weight(order[4], 4)
    add_pair(order[3], 3)
    grow_mixed(order[4])
    for copy in on_across:
        copy.wait_recv()
    grow_weight(order[5], 5)
    add_pair(order[4], 4)
    grow_mixed(order[5])
    for copy in p_right:
        copy.wait_recv()
    grow_weight(order[6], 6)
    add_pair(order[5], 5)
    for copy in p_left:
        copy.wait_recv()
    grow_weight(order[7], 7)
    add_pair(order[6], 6)
    grow_mixed(order[6])
    add_pair(order[7], 7)
    grow_mixed(order[7])

    @pl.loop(0, 4)
    def _(r):
        rows = pl.ds(pl.multiple_of(r * HALF, HALF), HALF)
        e[rows, :] = acc[rows, :].astype(BF)

    @pl.loop(0, NH)
    def _(h):
        for b in range(2):
            rl[b * NH + h] = mm(qst[b * NH + h], e[b * BLK : (b + 1) * BLK, cols(h)])
        whole = jnp.exp(total_of(h)) * rl[NH + h] + rl[h]
        for u in range(4):
            tx_r[h * 4 + u] = whole[32 * u : 32 * u + 32].astype(BF)

    r_first = exchange(tx_r, rx_r, 2)
    rx_r[tm] = tx_r[tm]

    def local_grads(h):
        for b in range(2):
            p = b * NH + h
            rows = slice(b * BLK, (b + 1) * BLK)
            eb = e[rows, cols(h)]
            qb = q[rows, cols(h)]
            kb = k[rows, cols(h)]
            vb = v[rows, cols(h)]
            lo, hi = slice(0, HALF), slice(HALF, BLK)
            bk = []
            for n, (ti, si) in enumerate(((lo, lo), (hi, lo), (hi, hi))):
                bk.append((mask[p, n] * mm_nt(eb[ti], vb[si])).astype(BF))
            near = jnp.concatenate(
                [mm(bk[0], kb[lo]), mm(bk[1], kb[lo]) + mm(bk[2], kb[hi])], axis=0
            )
            dq_ref[rows, cols(h)] = (near + ecol[p] * mm_nt(eb, sb[p])).astype(BF)
            acc[b * BLK : b * BLK + HALF, cols(h)] = mm_tn(bk[0], qb[lo]) + mm_tn(bk[1], qb[hi])
            acc[b * BLK + HALF : (b + 1) * BLK, cols(h)] = mm_tn(bk[2], qb[hi])
            dvp[b * BLK : b * BLK + HALF, cols(h)] = mm_tn(wts[p, 0], eb[lo]) + mm_tn(
                wts[p, 1], eb[hi]
            )
            dvp[b * BLK + HALF : (b + 1) * BLK, cols(h)] = mm_tn(wts[p, 2], eb[hi])

    @pl.loop(0, 2)
    def _(h):
        local_grads(h)

    for copy in r_first:
        copy.wait_recv()
    part = jnp.zeros((32, DK), F32)
    for i in reversed(range(TM)):
        tx_o[i] = part.astype(BF)
        part = jnp.concatenate([dec[i]] * 4, axis=0) * part + rx_r[i].astype(F32)
    r_second = exchange(tx_o, rx_o, 3)
    rx_o[tm] = tx_o[tm]

    def y_arrivals(part_z):
        for d in range(1, 4):
            pltpu.make_async_remote_copy(
                src_ref=y_tx.at[0],
                dst_ref=y_rx.at[0],
                send_sem=y_send.at[0],
                recv_sem=y_recv.at[part_z * 4 + d],
                device_id={"tm": mate},
                device_id_type=MESH,
            ).wait_recv()

    def y_sum(part_z, rows):
        total = y_rx[part_z * 4, rows].astype(F32)
        for i in range(1, 4):
            total = total + y_rx[part_z * 4 + i, rows].astype(F32)
        return total

    y_arrivals(1 - zl)

    @pl.loop(0, 2)
    def _(r):
        rows = pl.ds(pl.multiple_of(r * HALF, HALF), HALF)
        z_tx[rows, :] = y_sum(1 - zl, rows).astype(BF)

    z_copy = send(z_tx, z_rx, z_send.at[0], z_recv.at[0], {"tm": z_mate})

    @pl.loop(2, NH)
    def _(h):
        local_grads(h)

    y_arrivals(zl)
    for copy in r_second:
        copy.wait_recv()

    @pl.loop(0, NH)
    def _(h):
        end = rx_o[pl.ds(h * 4, 4)].reshape(DK, DK).astype(F32)
        ends = (jnp.exp(total_of(NH + h)) * end + rl[NH + h], end)
        for b in range(2):
            p = b * NH + h
            rows = slice(b * BLK, (b + 1) * BLK)
            carried = ends[b].astype(BF)
            dk_ref[rows, cols(h)] = (
                acc[rows, cols(h)] + fcol[p] * mm_nt(v[rows, cols(h)], carried)
            ).astype(BF)
            dv_ref[rows, cols(h)] = (
                dvp[rows, cols(h)] + fcol[p] * mm(k[rows, cols(h)], carried)
            ).astype(BF)

    z_copy.wait_recv()
    for r in range(2):
        rows = slice(r * HALF, (r + 1) * HALF)
        total = y_sum(zl, rows) + z_rx[rows, :].astype(F32)
        gw_ref[:, rows] = jnp.transpose(total)

    for n in range(8):
        gap, copy = y_copy(order[n], n)

        @pl.when(gap != 0)
        def _():
            copy.wait_send()

    for copy in sent:
        copy.wait_send()


def per_device(q, k, v, g, w, periods, log_decay):
    anywhere = pl.BlockSpec(memory_space=pl.ANY)
    vmem = pl.BlockSpec(memory_space=pltpu.VMEM)
    dma = pltpu.SemaphoreType.DMA
    return pl.pallas_call(
        kernel,
        out_shape=(
            jax.ShapeDtypeStruct((ROWS, NH * DK), BF),
            jax.ShapeDtypeStruct((ROWS, NH * DK), BF),
            jax.ShapeDtypeStruct((ROWS, NH * DK), BF),
            jax.ShapeDtypeStruct((HALF, NH * DK), F32),
        ),
        in_specs=[pl.BlockSpec(memory_space=pltpu.SMEM), vmem] + [anywhere] * 5,
        out_specs=[vmem] * 4,
        scratch_shapes=[
            pltpu.VMEM((ROWS, 512), BF),
            pltpu.VMEM((ROWS, 512), BF),
            pltpu.VMEM((ROWS, 512), BF),
            pltpu.VMEM((ROWS, 512), BF),
            pltpu.VMEM((8, ROWS, 512), BF),
            pltpu.VMEM((8, 512, 512), BF),
            pltpu.VMEM((ROWS, 512), F32),
            pltpu.VMEM((8, BLK), F32),
            pltpu.VMEM((8, BLK), F32),
            pltpu.VMEM((8, BLK, DK), F32),
            pltpu.VMEM((8, BLK, DK), F32),
            pltpu.VMEM((8, 3, HALF, HALF), F32),
            pltpu.VMEM((8, 3, HALF, HALF), BF),
            pltpu.VMEM((8, DK, BLK), BF),
            pltpu.VMEM((512, ROWS), BF),
            pltpu.VMEM((8, DK, DK), F32),
            pltpu.VMEM((8, DK, DK), BF),
            pltpu.VMEM((8, DK, DK), F32),
            pltpu.VMEM((ROWS, 512), F32),
            pltpu.VMEM((TM, 40, DK), F32),
            pltpu.VMEM((TM, 40, DK), F32),
            pltpu.VMEM((TM, 32, DK), BF),
            pltpu.VMEM((TM, 32, DK), BF),
            pltpu.VMEM((TM, 32, DK), BF),
            pltpu.VMEM((TM, 32, DK), BF),
            pltpu.VMEM((TM, 32, DK), BF),
            pltpu.VMEM((TM, 32, DK), BF),
            pltpu.VMEM((TM, 8, DK), F32),
            pltpu.VMEM((8, 512, HALF), BF),
            pltpu.VMEM((8, 512, HALF), BF),
            pltpu.VMEM((4, 512, HALF), F32),
            pltpu.VMEM((8, 512, HALF), BF),
            pltpu.VMEM((8, 512, HALF), BF),
            pltpu.VMEM((512, HALF), BF),
            pltpu.VMEM((512, HALF), BF),
            dma((5,)),
            dma((18,)),
            dma((18,)),
            dma((15,)),
            dma((15,)),
            dma((64,)),
            dma((64,)),
            dma((8,)),
            dma((8,)),
            dma((8,)),
            dma((8,)),
            dma((1,)),
            dma((1,)),
        ],
        compiler_params=pltpu.CompilerParams(
            collective_id=0, has_side_effects=True, vmem_limit_bytes=66_000_000
        ),
    )(periods, log_decay, q, k, v, g, w)


def solution(mesh):
    return jax.shard_map(
        per_device,
        mesh=mesh,
        in_specs=(
            P("tm", "head"),
            P("tm", "head"),
            P("tm", "head"),
            P("tm", "head"),
            P("tm", "head"),
            P("head"),
            P("head", "tm"),
        ),
        out_specs=(P("tm", "head"), P("tm", "head"), P("tm", "head"), P("tm", "head")),
        check_vma=False,
    )
```

time: 389 us -> 131 us (0.34); the launches traced: 383 us -> 129 us
  waiting for transfers between devices: 136 us -> 0 us
  Pallas kernels: 0 us -> 122 us
  matrix products: 69 us -> 0 us
  other arithmetic: 67.4 us -> 0 us
  local copies, waits for them, and re-layouts: 66.2 us -> 6.15 us
  blocking collectives: 28.8 us -> 0 us
  between operations: 14.6 us -> 0.65 us
    pallas_call x0 -> x1, Pallas kernels: none -> 122 us  [per_device(): pl.pallas_call(kernel, out_shape=(jax.ShapeDtypeStruct((ROWS, NH * DK), B...]
    all_gather x4 -> x0, waiting for transfers between devices: 120 us -> none  [the longest x1 99.7 us: per_device(): full_grad = lax.all_gather(grad_out, 'head', axis=1, tiled=True)]
    dot_general x26 -> x0, matrix products: 69 us -> none  [the longest x1 10.2 us: per_device(): lax.dot_general(columns, mixed_rows, (((0,), (0,)), ((), ())), preferred_...]
    select_n x33 -> x0, other arithmetic: 45.4 us -> none  [the longest x32 44.7 us: turn(): return jax.tree.map(lambda a, b: jnp.where(reached, a, b), new, before)]
    unnamed x1 -> x0, blocking collectives: 28.8 us -> none
    dynamic_update_slice x14 -> x0, local copies, waits for them, and re-layouts: 16.8 us -> none  [per_device(): mixed, weight_blocks, backed_blocks = lax.map(forward_output, sections[:7])]
    reduce_scatter x1 -> x0, waiting for transfers between devices: 14 us -> none  [per_device(): lax.psum_scatter(lax.dot_general(columns, mixed_rows, (((0,), (0,)), ((),...]
    while x25 -> x0, local copies, waits for them, and re-layouts: 8.08 us -> none  [the longest x2 4.05 us: per_device(): lax.map(gradient_output, sections + (weight_blocks, backed_blocks))]
  transfers between devices with their start and end apart: 5 -> 0, of which waited for: 4 -> 0; matrix products, arithmetic and copies ran while one was open for 34% -> 0% of each run, Pallas kernels for 0% -> 0%
where the time goes in v1:
time: 131 us; the launch traced here: 129 us
  Pallas kernels  122 us (93%)
  local copies, waits for them, and re-layouts  6.15 us (5%)
    pallas_call x1, Pallas kernels, per_device(): pl.pallas_call(kernel, out_shape=(jax.ShapeDtypeStruct((ROWS, NH * DK), B...  122 us
    unnamed x10, local copies, waits for them, and re-layouts  6.15 us

profile of v1, /device:TPU:1, one launch (start us, length us, event | category | flops | bytes accessed | tf_op | source)
XLA Modules:
  0.0 129.1 jit_solution(16436816339467587620)
XLA Ops:
  0.6 122.3 %shard_map.102 = (bf16[1024,512]{1,0:T(8,128)(2,1)}, bf16[1024,512]{1,0:T(8,128)(2,1)}, bf16[1024,512]{1,0:T(8,128)(2,1)}, f32[256,512]{1,0:T(8,128)}) custom-call(s32[4]{0:T(128)} %per_ref.1, f32[4,1024]{1,0:T(4,128)} %ld_ref.1, bf16[1024,512]{1,0:T(8,128)(2,1)} %q_hbm.1, bf16[1024,512]{1,0:T(8,128)(2,1)} %k_hbm.1, bf16[1024,512]{1,0:T(8,128)(2,1)} %v_hbm.1, ...), custom_call_target="tpu_custom_call" | custom-call | tf_op jit(solution)/shard_map/pallas_call | solution.py:555
  122.9 0.0 copy-start.1
  122.9 2.4 %copy.15 = bf16[1024,512]{1,0:T(8,128)(2,1)} copy(bf16[1024,512]{1,0:T(8,128)(2,1)} %get-tuple-element.8) | data formatting | bytes 2097152
  125.3 0.0 copy-done.1
  125.3 0.0 copy-start
  125.3 1.0 copy.16
  126.2 0.6 copy-done
  126.9 0.0 copy-start.2
  126.9 1.0 copy.17
  127.8 0.4 copy-done.2
  128.3 0.8 copy.18
Async XLA Ops:
  122.9 2.4 %copy-start.1 = (bf16[1024,512]{1,0:T(8,128)(2,1)S(1)}, bf16[1024,512]{1,0:T(8,128)(2,1)}, u32[]{:S(2)}) copy-start(bf16[1024,512]{1,0:T(8,128)(2,1)} %get-tuple-element.9) | copy-start | bytes 3145732
  125.3 1.6 %copy-start = (bf16[1024,512]{1,0:T(8,128)(2,1)S(1)}, bf16[1024,512]{1,0:T(8,128)(2,1)}, u32[]{:S(2)}) copy-start(bf16[1024,512]{1,0:T(8,128)(2,1)} %get-tuple-element.10) | copy-start | bytes 3145732
  126.9 1.4 %copy-start.2 = (f32[256,512]{1,0:T(8,128)S(1)}, f32[256,512]{1,0:T(8,128)}, u32[]{:S(2)}) copy-start(f32[256,512]{1,0:T(8,128)} %get-tuple-element.11) | copy-start | bytes 1572868

commit v2 on v1

--- a/solution.py
+++ b/solution.py
@@ -113,11 +113,12 @@
         return pltpu.make_async_copy(src, dst, load_sem.at[i])
 
     loads = [
-        local(q_hbm, q, 0),
-        local(k_hbm, k, 1),
-        local(v_hbm, v, 2),
-        local(g_hbm, grads.at[hd], 3),
-        local(w_hbm, weight.at[tm // 2, pl.ds(core * HALF, HALF)], 4),
+        local(k_hbm, k, 0),
+        local(v_hbm, v, 1),
+        local(q_hbm, q, 2),
+        local(g_hbm.at[:, 0:HALF], grads.at[hd, 0], 3),
+        local(g_hbm.at[:, HALF:512], grads.at[hd, 1], 4),
+        local(w_hbm, weight.at[tm // 2, pl.ds(core * HALF, HALF)], 5),
     ]
     for item in loads:
         item.start()
@@ -146,19 +147,24 @@
         sent.append(copy)
         return copy
 
-    def gather(src, slot, first, count, peer, n):
+    def gather(src, slot, c, first, count, peer, n):
         rows = pl.ds(first, count)
+        if src is g_hbm:
+            block = g_hbm.at[:, c * HALF : (c + 1) * HALF]
+        else:
+            block = grads.at[slot, c]
         return send(
-            src.at[rows],
-            grads.at[slot, rows],
+            block.at[rows],
+            grads.at[slot, c, rows],
             ag_send.at[n],
             ag_recv.at[n],
             {"head": peer},
         )
 
-    to_right = [gather(g_hbm, hd, c * 512, 512, right, c) for c in range(2)]
-    to_left = [gather(g_hbm, hd, c * 512, 512, left, 2 + c) for c in range(2)]
-    to_across = [gather(g_hbm, hd, 0, 512, across, 4)]
+    to_right, to_left = [], []
+    for c in range(2):
+        to_right.append(gather(g_hbm, hd, c, 0, ROWS, right, c))
+        to_left.append(gather(g_hbm, hd, c, 0, ROWS, left, 2 + c))
 
     def w_copy(src, owner, device, n):
         return send(
@@ -202,8 +208,8 @@
     def cols(h):
         return pl.ds(pl.multiple_of(h * DK, DK), DK)
 
-    for i in range(3):
-        loads[i].wait()
+    loads[0].wait()
+    loads[1].wait()
 
     @pl.loop(0, NH)
     def _(h):
@@ -232,12 +238,12 @@
 
     s_first = exchange(tx_s, rx_s, 0)
     rx_s[tm] = tx_s[tm]
-    to_across.append(gather(g_hbm, hd, 512, 512, across, 5))
     w_across = w_copy(w_hbm, tm, tm_at(1 - zl, y, core), 0)
     w_near = [
         w_copy(w_hbm, tm, tm_at(zl, lax.rem(y + d, 4), core), d) for d in range(1, 4)
     ]
     w_pair = [w_copy(w_hbm, tm, mate, 7)]
+    loads[2].wait()
 
     @pl.loop(0, NH)
     def _(h):
@@ -263,23 +269,6 @@
                 score = mm_nt(qb[ti * HALF : (ti + 1) * HALF], kb[si * HALF : (si + 1) * HALF])
                 wts[p, n] = (tile * score).astype(BF)
 
-    w_across.wait_recv()
-    z_mate = tm_at(1 - zl, y, core)
-    w_far = [
-        w_copy(w_block(z_mate), z_mate, tm_at(zl, lax.rem(y + d, 4), core), 3 + d)
-        for d in range(1, 4)
-    ]
-    w_pair.append(w_copy(w_block(z_mate), z_mate, mate, 8))
-    on_right, on_left = [], []
-
-    def pass_x(c):
-        to_right[c].wait_recv()
-        on_right.append(gather(grads.at[left], left, c * 512, 256, right, 6 + c))
-        to_left[c].wait_recv()
-        on_left.append(gather(grads.at[right], right, c * 512 + 256, 256, left, 8 + c))
-
-    pass_x(0)
-
     for copy in s_first:
         copy.wait_recv()
     part = jnp.zeros((32, DK), F32)
@@ -290,24 +279,39 @@
         part = jnp.concatenate([fall] * 4, axis=0) * part + rx_s[i, 0:32]
     s_second = exchange(tx_p, rx_p, 1)
     rx_p[tm] = tx_p[tm]
-
-    for d in range(1, 4):
-        src = tm_at(zl, lax.rem(y + 4 - d, 4), core)
-        w_near[d - 1].wait_recv()
-        w_pair.append(w_copy(w_block(src), src, mate, 8 + d))
-    pass_x(1)
+    to_across = [gather(g_hbm, hd, c, 0, ROWS, across, 4 + c) for c in range(2)]
+
+    w_across.wait_recv()
+    z_mate = tm_at(1 - zl, y, core)
+    w_far = [
+        w_copy(w_block(z_mate), z_mate, tm_at(zl, lax.rem(y + d, 4), core), 3 + d)
+        for d in range(1, 4)
+    ]
+    w_pair.append(w_copy(w_block(z_mate), z_mate, mate, 8))
+    on_right, on_left = [], []
+
+    def pass_x(c):
+        to_right[c].wait_recv()
+        on_right.append(gather(grads, left, c, 0, 512, right, 6 + c))
+        to_left[c].wait_recv()
+        on_left.append(gather(grads, right, c, 512, 512, left, 8 + c))
+
     p_right, p_left = [], []
 
     def pass_z(c):
         to_across[c].wait_recv()
-        p_right.append(gather(grads.at[across], across, c * 512, 512, right, 10 + c))
-        p_left.append(gather(grads.at[across], across, c * 512, 512, left, 12 + c))
-
-    pass_z(0)
-    for d in range(1, 4):
-        src = tm_at(1 - zl, lax.rem(y + 4 - d, 4), core)
-        w_far[d - 1].wait_recv()
-        w_pair.append(w_copy(w_block(src), src, mate, 11 + d))
+        p_right.append(gather(grads, across, c, 0, ROWS, right, 10 + c))
+        p_left.append(gather(grads, across, c, 0, ROWS, left, 12 + c))
+
+    on_across = []
+
+    def pass_far(c):
+        on_right[c].wait_recv()
+        on_across.append(gather(grads, far, c, 0, 512, across, 14 + 2 * c))
+        on_left[c].wait_recv()
+        on_across.append(gather(grads, far, c, 512, 512, across, 15 + 2 * c))
+
+    pass_x(0)
 
     for copy in s_second:
         copy.wait_recv()
@@ -329,106 +333,119 @@
             mixed = within + ecol[p] * mm(q[rows, cols(h)], state)
             mixt[cols(h), rows] = jnp.transpose(mixed).astype(BF)
 
-    pass_z(1)
-    on_across = []
-
-    def pass_far(c):
-        on_right[c].wait_recv()
-        on_across.append(gather(grads.at[far], far, c * 512, 256, across, 14 + 2 * c))
-        on_left[c].wait_recv()
-        on_across.append(gather(grads.at[far], far, c * 512 + 256, 256, across, 15 + 2 * c))
-
-    pass_far(0)
-
     @pl.loop(0, 4)
     def _(r):
         acc[pl.ds(r * HALF, HALF), :] = jnp.zeros((HALF, NH * DK), F32)
 
-    def grow_mixed(s):
+    def w_rows(s, c):
+        return weight[s, c * HALF : (c + 1) * HALF, :]
+
+    def grow_mixed(*units):
         @pl.loop(0, 4)
         def _(r):
             rows = pl.ds(pl.multiple_of(r * HALF, HALF), HALF)
-            acc[rows, :] += mm(grads[s, rows, :], weight[s])
+            total = acc[rows, :]
+            for s, c in units:
+                total = total + mm(grads[s, c, rows, :], w_rows(s, c))
+            acc[rows, :] = total
 
     mine = pl.ds(pl.multiple_of(core * HALF, HALF), HALF)
     other = pl.ds(pl.multiple_of((1 - core) * HALF, HALF), HALF)
+    units = []
     pairs = []
-
-    def grow_weight(s, n):
-        @pl.loop(0, 2)
-        def _(r):
-            rows = pl.ds(pl.multiple_of(r * HALF, HALF), HALF)
-            pair_tx[n, rows, :] = mm(mixt[rows, :], grads[s, :, other]).astype(BF)
-
+    y_sent = []
+
+    def grow_weight(s, c):
+        n = len(units)
+        units.append((s, c))
+        pair_tx[n] = mm(mixt[other, :], grads[s, c]).astype(BF)
         pairs.append(
             send(pair_tx.at[n], pair_rx.at[n], c_send.at[n], c_recv.at[n], {"tm": mate})
         )
-
-        @pl.loop(0, 2)
-        def _(r):
-            rows = pl.ds(pl.multiple_of(r * HALF, HALF), HALF)
-            pair_own[n % 4, rows, :] = mm(mixt[rows, :], grads[s, :, mine])
-
-    def y_copy(s, n):
-        gap = lax.rem(lax.rem(s, 4) + 4 - y, 4)
-        slot = (s // 4) * 4
-        return gap, pltpu.make_async_remote_copy(
-            src_ref=y_tx.at[n],
-            dst_ref=y_rx.at[slot + y],
-            send_sem=y_send.at[n],
-            recv_sem=y_recv.at[slot + gap],
-            device_id={"tm": tm_at(zl, lax.rem(s, 4), core)},
-            device_id_type=MESH,
-        )
-
-    def add_pair(s, n):
-        pairs[n].wait_recv()
-        y_tx[n] = (pair_own[n % 4] + pair_rx[n].astype(F32)).astype(BF)
-        gap, copy = y_copy(s, n)
-
-        @pl.when(gap != 0)
-        def _():
-            copy.start()
-
-        @pl.when(gap == 0)
-        def _():
-            y_rx[(s // 4) * 4 + y] = y_tx[n]
+        pair_own[n % 8] = mm(mixt[mine, :], grads[s, c])
+
+    def add_pairs():
+        for n in range(len(y_sent), len(units)):
+            s, c = units[n]
+            pairs[n].wait_recv()
+            y_tx[n] = (pair_own[n % 8] + pair_rx[n].astype(F32)).astype(BF)
+            gap = lax.rem(lax.rem(s, 4) + 4 - y, 4)
+            part_z = s // 4
+            copy = pltpu.make_async_remote_copy(
+                src_ref=y_tx.at[n],
+                dst_ref=y_rx.at[part_z, y, core],
+                send_sem=y_send.at[n],
+                recv_sem=y_recv.at[part_z, gap, core],
+                device_id={"tm": tm_at(zl, lax.rem(s, 4), c)},
+                device_id_type=MESH,
+            )
+            away = jnp.logical_or(gap != 0, core != c)
+
+            @pl.when(away)
+            def _():
+                copy.start()
+
+            @pl.when(jnp.logical_not(away))
+            def _():
+                y_rx[part_z, y, core] = y_tx[n]
+
+            y_sent.append((away, copy))
 
     z_right = lax.rem(right + 4, 8)
     z_left = lax.rem(left + 4, 8)
     z_far = lax.rem(far + 4, 8)
-    order = [hd, right, left, across, far, z_far, z_left, z_right]
 
     loads[3].wait()
     loads[4].wait()
+    grow_weight(hd, 0)
+    grow_weight(hd, 1)
+    pass_x(1)
+    pass_z(0)
+    add_pairs()
+    for c in range(2):
+        grow_weight(left, c)
+        grow_weight(right, c)
+    for d in range(1, 4):
+        src = tm_at(zl, lax.rem(y + 4 - d, 4), core)
+        w_near[d - 1].wait_recv()
+        w_pair.append(w_copy(w_block(src), src, mate, 8 + d))
+    add_pairs()
+    pass_far(0)
+    grow_weight(across, 0)
+    grow_weight(far, 0)
+    pass_z(1)
+    add_pairs()
+    grow_weight(across, 1)
+    for d in range(1, 4):
+        src = tm_at(1 - zl, lax.rem(y + 4 - d, 4), core)
+        w_far[d - 1].wait_recv()
+        w_pair.append(w_copy(w_block(src), src, mate, 11 + d))
+    pass_far(1)
+    grow_weight(far, 1)
+    add_pairs()
+    loads[5].wait()
     for copy in w_pair:
         copy.wait_recv()
-    grow_weight(order[0], 0)
-    grow_mixed(order[0])
-    pass_far(1)
-    for n in range(1, 4):
-        grow_weight(order[n], n)
-        add_pair(order[n - 1], n - 1)
-        grow_mixed(order[n])
-    grow_weight(order[4], 4)
-    add_pair(order[3], 3)
-    grow_mixed(order[4])
-    for copy in on_across:
+    grow_mixed(*units[0:5])
+    grow_mixed(*units[5:10])
+    for copy in (p_right[0], p_left[0], on_across[0], on_across[1]):
         copy.wait_recv()
-    grow_weight(order[5], 5)
-    add_pair(order[4], 4)
-    grow_mixed(order[5])
-    for copy in p_right:
+    grow_weight(z_left, 0)
+    grow_weight(z_right, 0)
+    grow_weight(z_far, 0)
+    grow_mixed(*units[10:13])
+    add_pairs()
+    for copy in (on_across[2], on_across[3]):
         copy.wait_recv()
-    grow_weight(order[6], 6)
-    add_pair(order[5], 5)
-    for copy in p_left:
-        copy.wait_recv()
-    grow_weight(order[7], 7)
-    add_pair(order[6], 6)
-    grow_mixed(order[6])
-    add_pair(order[7], 7)
-    grow_mixed(order[7])
+    grow_weight(z_far, 1)
+    grow_mixed(units[13])
+    add_pairs()
+    p_right[1].wait_recv()
+    p_left[1].wait_recv()
+    grow_weight(z_left, 1)
+    grow_weight(z_right, 1)
+    grow_mixed(*units[14:16])
+    add_pairs()
 
     @pl.loop(0, 4)
     def _(r):
@@ -483,28 +500,31 @@
     rx_o[tm] = tx_o[tm]
 
     def y_arrivals(part_z):
-        for d in range(1, 4):
+        def arrive(gap, half):
             pltpu.make_async_remote_copy(
                 src_ref=y_tx.at[0],
-                dst_ref=y_rx.at[0],
+                dst_ref=y_rx.at[0, 0, 0],
                 send_sem=y_send.at[0],
-                recv_sem=y_recv.at[part_z * 4 + d],
+                recv_sem=y_recv.at[part_z, gap, half],
                 device_id={"tm": mate},
                 device_id_type=MESH,
             ).wait_recv()
 
-    def y_sum(part_z, rows):
-        total = y_rx[part_z * 4, rows].astype(F32)
+        for gap in range(1, 4):
+            for half in range(2):
+                arrive(gap, half)
+        arrive(0, 1 - core)
+
+    def y_sum(part_z, half):
+        total = y_rx[part_z, 0, half].astype(F32)
         for i in range(1, 4):
-            total = total + y_rx[part_z * 4 + i, rows].astype(F32)
+            total = total + y_rx[part_z, i, half].astype(F32)
         return total
 
     y_arrivals(1 - zl)
 
-    @pl.loop(0, 2)
-    def _(r):
-        rows = pl.ds(pl.multiple_of(r * HALF, HALF), HALF)
-        z_tx[rows, :] = y_sum(1 - zl, rows).astype(BF)
+    for r in range(2):
+        z_tx[r * HALF : (r + 1) * HALF, :] = y_sum(1 - zl, r).astype(BF)
 
     z_copy = send(z_tx, z_rx, z_send.at[0], z_recv.at[0], {"tm": z_mate})
 
@@ -534,13 +554,12 @@
     z_copy.wait_recv()
     for r in range(2):
         rows = slice(r * HALF, (r + 1) * HALF)
-        total = y_sum(zl, rows) + z_rx[rows, :].astype(F32)
+        total = y_sum(zl, r) + z_rx[rows, :].astype(F32)
         gw_ref[:, rows] = jnp.transpose(total)
 
-    for n in range(8):
-        gap, copy = y_copy(order[n], n)
-
-        @pl.when(gap != 0)
+    for away, copy in y_sent:
+
+        @pl.when(away)
         def _():
             copy.wait_send()
 
@@ -567,7 +586,7 @@
             pltpu.VMEM((ROWS, 512), BF),
             pltpu.VMEM((ROWS, 512), BF),
             pltpu.VMEM((ROWS, 512), BF),
-            pltpu.VMEM((8, ROWS, 512), BF),
+            pltpu.VMEM((8, 2, ROWS, HALF), BF),
             pltpu.VMEM((8, 512, 512), BF),
             pltpu.VMEM((ROWS, 512), F32),
             pltpu.VMEM((8, BLK), F32),
@@ -591,24 +610,24 @@
             pltpu.VMEM((TM, 32, DK), BF),
             pltpu.VMEM((TM, 32, DK), BF),
             pltpu.VMEM((TM, 8, DK), F32),
-            pltpu.VMEM((8, 512, HALF), BF),
-            pltpu.VMEM((8, 512, HALF), BF),
-            pltpu.VMEM((4, 512, HALF), F32),
-            pltpu.VMEM((8, 512, HALF), BF),
-            pltpu.VMEM((8, 512, HALF), BF),
+            pltpu.VMEM((16, HALF, HALF), BF),
+            pltpu.VMEM((16, HALF, HALF), BF),
+            pltpu.VMEM((8, HALF, HALF), F32),
+            pltpu.VMEM((16, HALF, HALF), BF),
+            pltpu.VMEM((2, 4, 2, HALF, HALF), BF),
             pltpu.VMEM((512, HALF), BF),
             pltpu.VMEM((512, HALF), BF),
-            dma((5,)),
+            dma((6,)),
             dma((18,)),
             dma((18,)),
             dma((15,)),
             dma((15,)),
             dma((64,)),
             dma((64,)),
-            dma((8,)),
-            dma((8,)),
-            dma((8,)),
-            dma((8,)),
+            dma((16,)),
+            dma((16,)),
+            dma((16,)),
+            dma((2, 4, 2)),
             dma((1,)),
             dma((1,)),
         ],

time: 131 us -> 102 us (0.78)
  Pallas kernels: 122 us -> 93.2 us
    pallas_call x1, Pallas kernels: 122 us -> 93.2 us  [per_device(): pl.pallas_call(kernel, out_shape=(jax.ShapeDtypeStruct((ROWS, NH * DK), B...]
where the time goes in v2:
time: 102 us; the launch traced here: 100 us
  Pallas kernels  93.2 us (91%)
  local copies, waits for them, and re-layouts  6.15 us (6%)
    pallas_call x1, Pallas kernels, per_device(): pl.pallas_call(kernel, out_shape=(jax.ShapeDtypeStruct((ROWS, NH * DK), B...  93.2 us
    unnamed x10, local copies, waits for them, and re-layouts  6.15 us

profile of v2, /device:TPU:1, one launch (start us, length us, event | category | flops | bytes accessed | tf_op | source)
XLA Modules:
  0.0 100.0 jit_solution(12167274664789732411)
XLA Ops:
  0.6 93.2 %shard_map.102 = (bf16[1024,512]{1,0:T(8,128)(2,1)}, bf16[1024,512]{1,0:T(8,128)(2,1)}, bf16[1024,512]{1,0:T(8,128)(2,1)}, f32[256,512]{1,0:T(8,128)}) custom-call(s32[4]{0:T(128)} %per_ref.1, f32[4,1024]{1,0:T(4,128)} %ld_ref.1, bf16[1024,512]{1,0:T(8,128)(2,1)} %q_hbm.1, bf16[1024,512]{1,0:T(8,128)(2,1)} %k_hbm.1, bf16[1024,512]{1,0:T(8,128)(2,1)} %v_hbm.1, ...), custom_call_target="tpu_custom_call" | custom-call | tf_op jit(solution)/shard_map/pallas_call | solution.py:574
  93.8 0.0 copy-start.1
  93.8 2.4 %copy.15 = bf16[1024,512]{1,0:T(8,128)(2,1)} copy(bf16[1024,512]{1,0:T(8,128)(2,1)} %get-tuple-element.8) | data formatting | bytes 2097152
  96.2 0.0 copy-done.1
  96.2 0.0 copy-start
  96.2 1.0 copy.16
  97.2 0.6 copy-done
  97.8 0.0 copy-start.2
  97.8 1.0 copy.17
  98.8 0.4 copy-done.2
  99.2 0.8 copy.18
Async XLA Ops:
  93.8 2.4 %copy-start.1 = (bf16[1024,512]{1,0:T(8,128)(2,1)S(1)}, bf16[1024,512]{1,0:T(8,128)(2,1)}, u32[]{:S(2)}) copy-start(bf16[1024,512]{1,0:T(8,128)(2,1)} %get-tuple-element.9) | copy-start | bytes 3145732
  96.2 1.6 %copy-start = (bf16[1024,512]{1,0:T(8,128)(2,1)S(1)}, bf16[1024,512]{1,0:T(8,128)(2,1)}, u32[]{:S(2)}) copy-start(bf16[1024,512]{1,0:T(8,128)(2,1)} %get-tuple-element.10) | copy-start | bytes 3145732
  97.8 1.4 %copy-start.2 = (f32[256,512]{1,0:T(8,128)S(1)}, f32[256,512]{1,0:T(8,128)}, u32[]{:S(2)}) copy-start(f32[256,512]{1,0:T(8,128)} %get-tuple-element.11) | copy-start | bytes 1572868

commit v3 on v2

--- a/solution.py
+++ b/solution.py
@@ -130,54 +130,6 @@
         )
     for peer in (right, left, across):
         pl.semaphore_signal(barrier, inc=1, device_id={"head": peer}, device_id_type=MESH)
-    pl.semaphore_wait(barrier, TM + 2)
-
-    sent = []
-
-    def send(src, dst, send_sem, recv_sem, device):
-        copy = pltpu.make_async_remote_copy(
-            src_ref=src,
-            dst_ref=dst,
-            send_sem=send_sem,
-            recv_sem=recv_sem,
-            device_id=device,
-            device_id_type=MESH,
-        )
-        copy.start()
-        sent.append(copy)
-        return copy
-
-    def gather(src, slot, c, first, count, peer, n):
-        rows = pl.ds(first, count)
-        if src is g_hbm:
-            block = g_hbm.at[:, c * HALF : (c + 1) * HALF]
-        else:
-            block = grads.at[slot, c]
-        return send(
-            block.at[rows],
-            grads.at[slot, c, rows],
-            ag_send.at[n],
-            ag_recv.at[n],
-            {"head": peer},
-        )
-
-    to_right, to_left = [], []
-    for c in range(2):
-        to_right.append(gather(g_hbm, hd, c, 0, ROWS, right, c))
-        to_left.append(gather(g_hbm, hd, c, 0, ROWS, left, 2 + c))
-
-    def w_copy(src, owner, device, n):
-        return send(
-            src,
-            weight.at[owner // 2, pl.ds(lax.rem(owner, 2) * HALF, HALF)],
-            w_send.at[n],
-            w_recv.at[n],
-            {"tm": device},
-        )
-
-    def w_block(owner):
-        return weight.at[owner // 2, pl.ds(lax.rem(owner, 2) * HALF, HALF)]
-
     ids = lax.broadcasted_iota(jnp.int32, (8, BLK), 0)
     lane = lax.broadcasted_iota(jnp.int32, (8, BLK), 1)
     head_of = lax.rem(ids, NH)
@@ -197,6 +149,55 @@
         shift *= 2
     cum[...] = run
     upd[...] = update
+
+    pl.semaphore_wait(barrier, TM + 2)
+
+    sent = []
+
+    def send(src, dst, send_sem, recv_sem, device):
+        copy = pltpu.make_async_remote_copy(
+            src_ref=src,
+            dst_ref=dst,
+            send_sem=send_sem,
+            recv_sem=recv_sem,
+            device_id=device,
+            device_id_type=MESH,
+        )
+        copy.start()
+        sent.append(copy)
+        return copy
+
+    def gather(src, slot, c, first, count, peer, n):
+        rows = pl.ds(first, count)
+        if src is g_hbm:
+            block = g_hbm.at[:, c * HALF : (c + 1) * HALF]
+        else:
+            block = grads.at[slot, c]
+        return send(
+            block.at[rows],
+            grads.at[slot, c, rows],
+            ag_send.at[n],
+            ag_recv.at[n],
+            {"head": peer},
+        )
+
+    to_right, to_left = [], []
+    for c in range(2):
+        to_right.append(gather(g_hbm, hd, c, 0, ROWS, right, c))
+        to_left.append(gather(g_hbm, hd, c, 0, ROWS, left, 2 + c))
+    to_across = [gather(g_hbm, hd, 0, 0, ROWS, across, 4)]
+
+    def w_copy(src, owner, device, n):
+        return send(
+            src,
+            weight.at[owner // 2, pl.ds(lax.rem(owner, 2) * HALF, HALF)],
+            w_send.at[n],
+            w_recv.at[n],
+            {"tm": device},
+        )
+
+    def w_block(owner):
+        return weight.at[owner // 2, pl.ds(lax.rem(owner, 2) * HALF, HALF)]
 
     def rows_of(p):
         return cum[pl.ds(p, 1), :], upd[pl.ds(p, 1), :]
@@ -279,8 +280,32 @@
         part = jnp.concatenate([fall] * 4, axis=0) * part + rx_s[i, 0:32]
     s_second = exchange(tx_p, rx_p, 1)
     rx_p[tm] = tx_p[tm]
-    to_across = [gather(g_hbm, hd, c, 0, ROWS, across, 4 + c) for c in range(2)]
-
+    to_across.append(gather(g_hbm, hd, 1, 0, ROWS, across, 5))
+
+    on_right, on_left = [], []
+
+    def pass_x(c):
+        to_right[c].wait_recv()
+        on_right.append(gather(grads, left, c, 0, 512, right, 6 + c))
+        to_left[c].wait_recv()
+        on_left.append(gather(grads, right, c, 512, 512, left, 8 + c))
+
+    p_right, p_left = [], []
+
+    def pass_z(c):
+        to_across[c].wait_recv()
+        p_right.append(gather(grads, across, c, 0, ROWS, right, 10 + c))
+        p_left.append(gather(grads, across, c, 0, ROWS, left, 12 + c))
+
+    on_across = []
+
+    def pass_far(c):
+        on_right[c].wait_recv()
+        on_across.append(gather(grads, far, c, 0, 512, across, 14 + 2 * c))
+        on_left[c].wait_recv()
+        on_across.append(gather(grads, far, c, 512, 512, across, 15 + 2 * c))
+
+    pass_x(0)
     w_across.wait_recv()
     z_mate = tm_at(1 - zl, y, core)
     w_far = [
@@ -288,30 +313,6 @@
         for d in range(1, 4)
     ]
     w_pair.append(w_copy(w_block(z_mate), z_mate, mate, 8))
-    on_right, on_left = [], []
-
-    def pass_x(c):
-        to_right[c].wait_recv()
-        on_right.append(gather(grads, left, c, 0, 512, right, 6 + c))
-        to_left[c].wait_recv()
-        on_left.append(gather(grads, right, c, 512, 512, left, 8 + c))
-
-    p_right, p_left = [], []
-
-    def pass_z(c):
-        to_across[c].wait_recv()
-        p_right.append(gather(grads, across, c, 0, ROWS, right, 10 + c))
-        p_left.append(gather(grads, across, c, 0, ROWS, left, 12 + c))
-
-    on_across = []
-
-    def pass_far(c):
-        on_right[c].wait_recv()
-        on_across.append(gather(grads, far, c, 0, 512, across, 14 + 2 * c))
-        on_left[c].wait_recv()
-        on_across.append(gather(grads, far, c, 512, 512, across, 15 + 2 * c))
-
-    pass_x(0)
 
     for copy in s_second:
         copy.wait_recv()
@@ -442,10 +443,7 @@
     add_pairs()
     p_right[1].wait_recv()
     p_left[1].wait_recv()
-    grow_weight(z_left, 1)
-    grow_weight(z_right, 1)
-    grow_mixed(*units[14:16])
-    add_pairs()
+    grow_mixed((z_left, 1), (z_right, 1))
 
     @pl.loop(0, 4)
     def _(r):
@@ -462,6 +460,9 @@
 
     r_first = exchange(tx_r, rx_r, 2)
     rx_r[tm] = tx_r[tm]
+    grow_weight(z_left, 1)
+    grow_weight(z_right, 1)
+    add_pairs()
 
     def local_grads(h):
         for b in range(2):
@@ -567,18 +568,44 @@
         copy.wait_send()
 
 
+def hand_over(*refs):
+    src, dst, held = refs[0:4], refs[4:8], refs[8:12]
+    sem_in, sem_out = refs[12:14]
+    pieces = []
+    for i in range(4):
+        count = 4 if i < 3 else 2
+        rows = src[i].shape[0] // count
+        for r in range(count):
+            at = pl.ds(r * rows, rows)
+            n = len(pieces)
+            pieces.append(
+                (
+                    pltpu.make_async_copy(src[i].at[at], held[i].at[at], sem_in.at[n]),
+                    pltpu.make_async_copy(held[i].at[at], dst[i].at[at], sem_out.at[n]),
+                )
+            )
+    for fetch, _ in pieces:
+        fetch.start()
+    for fetch, put in pieces:
+        fetch.wait()
+        put.start()
+    for _, put in pieces:
+        put.wait()
+
+
 def per_device(q, k, v, g, w, periods, log_decay):
     anywhere = pl.BlockSpec(memory_space=pl.ANY)
     vmem = pl.BlockSpec(memory_space=pltpu.VMEM)
     dma = pltpu.SemaphoreType.DMA
-    return pl.pallas_call(
+    shapes = (
+        jax.ShapeDtypeStruct((ROWS, NH * DK), BF),
+        jax.ShapeDtypeStruct((ROWS, NH * DK), BF),
+        jax.ShapeDtypeStruct((ROWS, NH * DK), BF),
+        jax.ShapeDtypeStruct((HALF, NH * DK), F32),
+    )
+    made = pl.pallas_call(
         kernel,
-        out_shape=(
-            jax.ShapeDtypeStruct((ROWS, NH * DK), BF),
-            jax.ShapeDtypeStruct((ROWS, NH * DK), BF),
-            jax.ShapeDtypeStruct((ROWS, NH * DK), BF),
-            jax.ShapeDtypeStruct((HALF, NH * DK), F32),
-        ),
+        out_shape=shapes,
         in_specs=[pl.BlockSpec(memory_space=pltpu.SMEM), vmem] + [anywhere] * 5,
         out_specs=[vmem] * 4,
         scratch_shapes=[
@@ -635,6 +662,13 @@
             collective_id=0, has_side_effects=True, vmem_limit_bytes=66_000_000
         ),
     )(periods, log_decay, q, k, v, g, w)
+    return pl.pallas_call(
+        hand_over,
+        out_shape=shapes,
+        in_specs=[anywhere] * 4,
+        out_specs=[anywhere] * 4,
+        scratch_shapes=[pltpu.VMEM(t.shape, t.dtype) for t in shapes] + [dma((14,)), dma((14,))],
+    )(*made)
 
 
 def solution(mesh):

time: 102 us -> 93.6 us (0.918)
  local copies, waits for them, and re-layouts: 6.15 us -> 0 us
  Pallas kernels: 93.2 us -> 91.6 us
    unnamed x10 -> x0, local copies, waits for them, and re-layouts: 6.15 us -> none
    pallas_call x1 -> x2, Pallas kernels: 93.2 us -> 91.6 us  [the longest x1 88.3 us: per_device(): pl.pallas_call(kernel, out_shape=shapes, in_specs=[pl.BlockSpec(memory_sp...]
where the time goes in v3:
time: 93.6 us; the launch traced here: 92.4 us
  Pallas kernels  91.6 us (98%)
    pallas_call x1, Pallas kernels, per_device(): pl.pallas_call(kernel, out_shape=shapes, in_specs=[pl.BlockSpec(memory_sp...  88.3 us
    pallas_call x1, Pallas kernels, per_device(): pl.pallas_call(hand_over, out_shape=shapes, in_specs=[anywhere] * 4, out_...  3.26 us

profile of v3, /device:TPU:1, one launch (start us, length us, event | category | flops | bytes accessed | tf_op | source)
XLA Modules:
  0.0 92.4 jit_solution(8321439891315678363)
XLA Ops:
  0.6 88.3 %shard_map.102 = (bf16[1024,512]{1,0:T(8,128)(2,1)}, bf16[1024,512]{1,0:T(8,128)(2,1)}, bf16[1024,512]{1,0:T(8,128)(2,1)}, f32[256,512]{1,0:T(8,128)}) custom-call(s32[4]{0:T(128)} %per_ref.1, f32[4,1024]{1,0:T(4,128)} %ld_ref.1, bf16[1024,512]{1,0:T(8,128)(2,1)} %q_hbm.1, bf16[1024,512]{1,0:T(8,128)(2,1)} %k_hbm.1, bf16[1024,512]{1,0:T(8,128)(2,1)} %v_hbm.1, ...), custom_call_target="tpu_custom_call" | custom-call | tf_op jit(solution)/shard_map/pallas_call | solution.py:606
  89.0 3.3 %shard_map.103 = (bf16[1024,512]{1,0:T(8,128)(2,1)}, bf16[1024,512]{1,0:T(8,128)(2,1)}, bf16[1024,512]{1,0:T(8,128)(2,1)}, f32[256,512]{1,0:T(8,128)}) custom-call(bf16[1024,512]{1,0:T(8,128)(2,1)} %get-tuple-element.8.refs_0_, bf16[1024,512]{1,0:T(8,128)(2,1)} %get-tuple-element.9.refs_1_, bf16[1024,512]{1,0:T(8,128)(2,1)} %get-tuple-element.10.refs_2_, ...), custom_call_target="tpu_custom_call" | custom-call | tf_op jit(solution)/shard_map/pallas_call | solution.py:665

commit v4 on v3

--- a/solution.py
+++ b/solution.py
@@ -40,6 +40,10 @@
     v_hbm,
     g_hbm,
     w_hbm,
+    dq_hbm,
+    dk_hbm,
+    dv_hbm,
+    gw_hbm,
     dq_ref,
     dk_ref,
     dv_ref,
@@ -79,6 +83,7 @@
     y_rx,
     z_tx,
     z_rx,
+    out_sem,
     load_sem,
     ag_send,
     ag_recv,
@@ -227,11 +232,13 @@
             tx_s[h * 4 + u, 0:32] = whole[32 * u : 32 * u + 32]
             tx_s[h * 4 + u, 32:40] = jnp.broadcast_to(t0 + t1, (8, DK))
 
+    steps = [(dz, dy, dc) for dz in (1, 0) for dy in (2, 1, 3, 0) for dc in (1, 0)][:-1]
+
     def exchange(tx, rx, kind):
         copies = []
-        for d in range(1, TM):
-            peer = lax.rem(tm + d, TM)
-            n = kind * TM + d
+        for n, (dz, dy, dc) in enumerate(steps):
+            peer = tm_at(lax.rem(zl + dz, 2), lax.rem(y + dy, 4), lax.rem(core + dc, 2))
+            n = kind * TM + n
             copies.append(
                 send(tx.at[peer], rx.at[tm], s_send.at[n], s_recv.at[n], {"tm": peer})
             )
@@ -341,14 +348,17 @@
     def w_rows(s, c):
         return weight[s, c * HALF : (c + 1) * HALF, :]
 
-    def grow_mixed(*units):
+    def grow_mixed(*units, last=False):
         @pl.loop(0, 4)
         def _(r):
             rows = pl.ds(pl.multiple_of(r * HALF, HALF), HALF)
             total = acc[rows, :]
             for s, c in units:
                 total = total + mm(grads[s, c, rows, :], w_rows(s, c))
-            acc[rows, :] = total
+            if last:
+                e[rows, :] = total.astype(BF)
+            else:
+                acc[rows, :] = total
 
     mine = pl.ds(pl.multiple_of(core * HALF, HALF), HALF)
     other = pl.ds(pl.multiple_of((1 - core) * HALF, HALF), HALF)
@@ -441,14 +451,51 @@
     grow_weight(z_far, 1)
     grow_mixed(units[13])
     add_pairs()
+    def y_arrivals(part_z):
+        def arrive(gap, half):
+            pltpu.make_async_remote_copy(
+                src_ref=y_tx.at[0],
+                dst_ref=y_rx.at[0, 0, 0],
+                send_sem=y_send.at[0],
+                recv_sem=y_recv.at[part_z, gap, half],
+                device_id={"tm": mate},
+                device_id_type=MESH,
+            ).wait_recv()
+
+        for gap in range(1, 4):
+            for half in range(2):
+                arrive(gap, half)
+        arrive(0, 1 - core)
+
+    def y_sum(part_z, half):
+        total = y_rx[part_z, 0, half].astype(F32)
+        for i in range(1, 4):
+            total = total + y_rx[part_z, i, half].astype(F32)
+        return total
+
+    z_copy = pltpu.make_async_remote_copy(
+        src_ref=z_tx,
+        dst_ref=z_rx,
+        send_sem=z_send.at[0],
+        recv_sem=z_recv.at[0],
+        device_id={"tm": z_mate},
+        device_id_type=MESH,
+    )
+    sent.append(z_copy)
+
+    def z_stage():
+        y_arrivals(1 - zl)
+        for r in range(2):
+            z_tx[r * HALF : (r + 1) * HALF, :] = y_sum(1 - zl, r).astype(BF)
+        z_copy.start()
+
+    @pl.when(core == 0)
+    def _():
+        z_stage()
+
     p_right[1].wait_recv()
     p_left[1].wait_recv()
-    grow_mixed((z_left, 1), (z_right, 1))
-
-    @pl.loop(0, 4)
-    def _(r):
-        rows = pl.ds(pl.multiple_of(r * HALF, HALF), HALF)
-        e[rows, :] = acc[rows, :].astype(BF)
+    grow_mixed((z_left, 1), (z_right, 1), last=True)
 
     @pl.loop(0, NH)
     def _(h):
@@ -500,40 +547,24 @@
     r_second = exchange(tx_o, rx_o, 3)
     rx_o[tm] = tx_o[tm]
 
-    def y_arrivals(part_z):
-        def arrive(gap, half):
-            pltpu.make_async_remote_copy(
-                src_ref=y_tx.at[0],
-                dst_ref=y_rx.at[0, 0, 0],
-                send_sem=y_send.at[0],
-                recv_sem=y_recv.at[part_z, gap, half],
-                device_id={"tm": mate},
-                device_id_type=MESH,
-            ).wait_recv()
-
-        for gap in range(1, 4):
-            for half in range(2):
-                arrive(gap, half)
-        arrive(0, 1 - core)
-
-    def y_sum(part_z, half):
-        total = y_rx[part_z, 0, half].astype(F32)
-        for i in range(1, 4):
-            total = total + y_rx[part_z, i, half].astype(F32)
-        return total
-
-    y_arrivals(1 - zl)
-
-    for r in range(2):
-        z_tx[r * HALF : (r + 1) * HALF, :] = y_sum(1 - zl, r).astype(BF)
-
-    z_copy = send(z_tx, z_rx, z_send.at[0], z_recv.at[0], {"tm": z_mate})
-
+    results = [
+        pltpu.make_async_copy(held, out, out_sem.at[i])
+        for i, (held, out) in enumerate(
+            ((dq_ref, dq_hbm), (dk_ref, dk_hbm), (dv_ref, dv_hbm), (gw_ref, gw_hbm))
+        )
+    ]
     @pl.loop(2, NH)
     def _(h):
         local_grads(h)
 
+    results[0].start()
+    @pl.when(core == 1)
+    def _():
+        z_stage()
+
     y_arrivals(zl)
+    for r in range(2):
+        pair_own[r] = y_sum(zl, r)
     for copy in r_second:
         copy.wait_recv()
 
@@ -552,11 +583,14 @@
                 dvp[rows, cols(h)] + fcol[p] * mm(k[rows, cols(h)], carried)
             ).astype(BF)
 
+    results[1].start()
+    results[2].start()
     z_copy.wait_recv()
     for r in range(2):
         rows = slice(r * HALF, (r + 1) * HALF)
-        total = y_sum(zl, r) + z_rx[rows, :].astype(F32)
+        total = pair_own[r] + z_rx[rows, :].astype(F32)
         gw_ref[:, rows] = jnp.transpose(total)
+    results[3].start()
 
     for away, copy in y_sent:
 
@@ -566,6 +600,8 @@
 
     for copy in sent:
         copy.wait_send()
+    for copy in results:
+        copy.wait()
 
 
 def hand_over(*refs):
@@ -607,8 +643,9 @@
         kernel,
         out_shape=shapes,
         in_specs=[pl.BlockSpec(memory_space=pltpu.SMEM), vmem] + [anywhere] * 5,
-        out_specs=[vmem] * 4,
-        scratch_shapes=[
+        out_specs=[anywhere] * 4,
+        scratch_shapes=[pltpu.VMEM(t.shape, t.dtype) for t in shapes]
+        + [
             pltpu.VMEM((ROWS, 512), BF),
             pltpu.VMEM((ROWS, 512), BF),
             pltpu.VMEM((ROWS, 512), BF),
@@ -644,6 +681,7 @@
             pltpu.VMEM((2, 4, 2, HALF, HALF), BF),
             pltpu.VMEM((512, HALF), BF),
             pltpu.VMEM((512, HALF), BF),
+            dma((4,)),
             dma((6,)),
             dma((18,)),
             dma((18,)),

time: 93.6 us -> 91.8 us (0.981)
  Pallas kernels: 91.6 us -> 90.2 us
    pallas_call x1, Pallas kernels: 88.3 us -> 86.9 us  [per_device(): pl.pallas_call(kernel, out_shape=shapes, in_specs=[pl.BlockSpec(memory_sp...]
where the time goes in v4:
time: 91.8 us; the launch traced here: 91 us
  Pallas kernels  90.2 us (98%)
    pallas_call x1, Pallas kernels, per_device(): pl.pallas_call(kernel, out_shape=shapes, in_specs=[pl.BlockSpec(memory_sp...  86.9 us
    pallas_call x1, Pallas kernels, per_device(): pl.pallas_call(hand_over, out_shape=shapes, in_specs=[anywhere] * 4, out_...  3.26 us

profile of v4, /device:TPU:1, one launch (start us, length us, event | category | flops | bytes accessed | tf_op | source)
XLA Modules:
  0.0 91.0 jit_solution(6807133817366919160)
XLA Ops:
  0.6 86.9 %shard_map.102 = (bf16[1024,512]{1,0:T(8,128)(2,1)}, bf16[1024,512]{1,0:T(8,128)(2,1)}, bf16[1024,512]{1,0:T(8,128)(2,1)}, f32[256,512]{1,0:T(8,128)}) custom-call(s32[4]{0:T(128)} %per_ref.1, f32[4,1024]{1,0:T(4,128)} %ld_ref.1, bf16[1024,512]{1,0:T(8,128)(2,1)} %q_hbm.1, bf16[1024,512]{1,0:T(8,128)(2,1)} %k_hbm.1, bf16[1024,512]{1,0:T(8,128)(2,1)} %v_hbm.1, ...), custom_call_target="tpu_custom_call" | custom-call | tf_op jit(solution)/shard_map/pallas_call | solution.py:642
  87.6 3.3 %shard_map.103 = (bf16[1024,512]{1,0:T(8,128)(2,1)}, bf16[1024,512]{1,0:T(8,128)(2,1)}, bf16[1024,512]{1,0:T(8,128)(2,1)}, f32[256,512]{1,0:T(8,128)}) custom-call(bf16[1024,512]{1,0:T(8,128)(2,1)} %get-tuple-element.8.refs_0_, bf16[1024,512]{1,0:T(8,128)(2,1)} %get-tuple-element.9.refs_1_, bf16[1024,512]{1,0:T(8,128)(2,1)} %get-tuple-element.10.refs_2_, ...), custom_call_target="tpu_custom_call" | custom-call | tf_op jit(solution)/shard_map/pallas_call | solution.py:703

commit v5 on v4

--- a/solution.py
+++ b/solution.py
@@ -299,10 +299,19 @@
 
     p_right, p_left = [], []
 
+    def quarter(slot, sub, peer, n):
+        block = grads.at[slot, 1, :, sub * DK : (sub + 1) * DK]
+        return send(block, block, ag_send.at[n], ag_recv.at[n], {"head": peer})
+
     def pass_z(c):
         to_across[c].wait_recv()
-        p_right.append(gather(grads, across, c, 0, ROWS, right, 10 + c))
-        p_left.append(gather(grads, across, c, 0, ROWS, left, 12 + c))
+        if c == 0:
+            p_right.append(gather(grads, across, c, 0, ROWS, right, 10))
+            p_left.append(gather(grads, across, c, 0, ROWS, left, 12))
+        else:
+            for sub in range(2):
+                p_right.append(quarter(across, sub, right, 18 + sub))
+                p_left.append(quarter(across, sub, left, 20 + sub))
 
     on_across = []
 
@@ -348,17 +357,14 @@
     def w_rows(s, c):
         return weight[s, c * HALF : (c + 1) * HALF, :]
 
-    def grow_mixed(*units, last=False):
+    def grow_mixed(*units):
         @pl.loop(0, 4)
         def _(r):
             rows = pl.ds(pl.multiple_of(r * HALF, HALF), HALF)
             total = acc[rows, :]
             for s, c in units:
                 total = total + mm(grads[s, c, rows, :], w_rows(s, c))
-            if last:
-                e[rows, :] = total.astype(BF)
-            else:
-                acc[rows, :] = total
+            acc[rows, :] = total
 
     mine = pl.ds(pl.multiple_of(core * HALF, HALF), HALF)
     other = pl.ds(pl.multiple_of((1 - core) * HALF, HALF), HALF)
@@ -375,32 +381,84 @@
         )
         pair_own[n % 8] = mm(mixt[mine, :], grads[s, c])
 
+    def y_put(s, c, m, sub):
+        gap = lax.rem(lax.rem(s, 4) + 4 - y, 4)
+        part_z = s // 4
+        at = pl.ds(sub * DK, DK) if c else pl.ds(0, HALF)
+        copy = pltpu.make_async_remote_copy(
+            src_ref=y_tx.at[m, :, at],
+            dst_ref=y_rx.at[part_z, y, core, :, at],
+            send_sem=y_send.at[2 * m + sub],
+            recv_sem=y_recv.at[part_z, gap, core, sub],
+            device_id={"tm": tm_at(zl, lax.rem(s, 4), c)},
+            device_id_type=MESH,
+        )
+        away = jnp.logical_or(gap != 0, core != c)
+
+        @pl.when(away)
+        def _():
+            copy.start()
+
+        @pl.when(jnp.logical_not(away))
+        def _():
+            y_rx[part_z, y, core, :, at] = y_tx[m, :, at]
+
+        y_sent.append((away, copy))
+
+    added = []
+
     def add_pairs():
-        for n in range(len(y_sent), len(units)):
+        for n in range(len(added), len(units)):
             s, c = units[n]
             pairs[n].wait_recv()
             y_tx[n] = (pair_own[n % 8] + pair_rx[n].astype(F32)).astype(BF)
-            gap = lax.rem(lax.rem(s, 4) + 4 - y, 4)
-            part_z = s // 4
-            copy = pltpu.make_async_remote_copy(
-                src_ref=y_tx.at[n],
-                dst_ref=y_rx.at[part_z, y, core],
-                send_sem=y_send.at[n],
-                recv_sem=y_recv.at[part_z, gap, core],
-                device_id={"tm": tm_at(zl, lax.rem(s, 4), c)},
-                device_id_type=MESH,
+            for sub in range(1 + c):
+                y_put(s, c, n, sub)
+            added.append(n)
+
+    def last_weight(sub):
+        at = pl.ds(sub * DK, DK)
+        block = jnp.concatenate([grads[z_left, 1, :, at], grads[z_right, 1, :, at]], axis=1)
+        part = mm(mixt[other, :], block).astype(BF)
+        copies = []
+        for i in range(2):
+            m, n = 14 + i, 14 + 2 * sub + i
+            pair_tx[m, :, at] = part[:, i * DK : (i + 1) * DK]
+            copies.append(
+                send(
+                    pair_tx.at[m, :, at],
+                    pair_rx.at[m, :, at],
+                    c_send.at[n],
+                    c_recv.at[n],
+                    {"tm": mate},
+                )
             )
-            away = jnp.logical_or(gap != 0, core != c)
-
-            @pl.when(away)
-            def _():
-                copy.start()
-
-            @pl.when(jnp.logical_not(away))
-            def _():
-                y_rx[part_z, y, core] = y_tx[n]
-
-            y_sent.append((away, copy))
+        part = mm(mixt[mine, :], block)
+        for i in range(2):
+            pair_own[6 + i, :, at] = part[:, i * DK : (i + 1) * DK]
+        return copies
+
+    def last_add(sub, copies):
+        at = pl.ds(sub * DK, DK)
+        for i, s in enumerate((z_left, z_right)):
+            copies[i].wait_recv()
+            y_tx[14 + i, :, at] = (
+                pair_own[6 + i, :, at] + pair_rx[14 + i, :, at].astype(F32)
+            ).astype(BF)
+            y_put(s, 1, 14 + i, sub)
+
+    def last_mixed(sub, dst):
+        at = pl.ds(sub * DK, DK)
+        deep = pl.ds(HALF + sub * DK, DK)
+        block = jnp.concatenate([weight[z_left, deep, :], weight[z_right, deep, :]], axis=0)
+
+        @pl.loop(0, 4)
+        def _(r):
+            rows = pl.ds(pl.multiple_of(r * HALF, HALF), HALF)
+            held = jnp.concatenate(
+                [grads[z_left, 1, rows, at], grads[z_right, 1, rows, at]], axis=1
+            )
+            dst[rows, :] = (acc[rows, :] + mm(held, block)).astype(dst.dtype)
 
     z_right = lax.rem(right + 4, 8)
     z_left = lax.rem(left + 4, 8)
@@ -451,51 +509,66 @@
     grow_weight(z_far, 1)
     grow_mixed(units[13])
     add_pairs()
-    def y_arrivals(part_z):
-        def arrive(gap, half):
+    def y_arrivals(part_z, c, subs):
+        def arrive(gap, half, sub):
+            at = pl.ds(sub * DK, DK) if c else pl.ds(0, HALF)
             pltpu.make_async_remote_copy(
-                src_ref=y_tx.at[0],
-                dst_ref=y_rx.at[0, 0, 0],
+                src_ref=y_tx.at[0, :, at],
+                dst_ref=y_rx.at[0, 0, 0, :, at],
                 send_sem=y_send.at[0],
-                recv_sem=y_recv.at[part_z, gap, half],
+                recv_sem=y_recv.at[part_z, gap, half, sub],
                 device_id={"tm": mate},
                 device_id_type=MESH,
             ).wait_recv()
 
-        for gap in range(1, 4):
-            for half in range(2):
-                arrive(gap, half)
-        arrive(0, 1 - core)
-
-    def y_sum(part_z, half):
-        total = y_rx[part_z, 0, half].astype(F32)
+        for sub in subs:
+            for gap in range(1, 4):
+                for half in range(2):
+                    arrive(gap, half, sub)
+            arrive(0, 1 - c, sub)
+
+    def y_sum(part_z, half, at=slice(None)):
+        total = y_rx[part_z, 0, half, :, at].astype(F32)
         for i in range(1, 4):
-            total = total + y_rx[part_z, i, half].astype(F32)
+            total = total + y_rx[part_z, i, half, :, at].astype(F32)
         return total
 
-    z_copy = pltpu.make_async_remote_copy(
-        src_ref=z_tx,
-        dst_ref=z_rx,
-        send_sem=z_send.at[0],
-        recv_sem=z_recv.at[0],
-        device_id={"tm": z_mate},
-        device_id_type=MESH,
-    )
-    sent.append(z_copy)
-
-    def z_stage():
-        y_arrivals(1 - zl)
-        for r in range(2):
-            z_tx[r * HALF : (r + 1) * HALF, :] = y_sum(1 - zl, r).astype(BF)
-        z_copy.start()
+    z_copies = []
+    for sub in range(2):
+        at = pl.ds(sub * DK, DK)
+        z_copies.append(
+            pltpu.make_async_remote_copy(
+                src_ref=z_tx.at[:, at],
+                dst_ref=z_rx.at[:, at],
+                send_sem=z_send.at[sub],
+                recv_sem=z_recv.at[sub],
+                device_id={"tm": z_mate},
+                device_id_type=MESH,
+            )
+        )
+    sent.extend(z_copies)
+
+    def z_stage(c, subs):
+        y_arrivals(1 - zl, c, subs if c else (0,))
+        for sub in subs:
+            at = pl.ds(sub * DK, DK)
+            for r in range(2):
+                z_tx[r * HALF : (r + 1) * HALF, at] = y_sum(1 - zl, r, at).astype(BF)
+            z_copies[sub].start()
+
+    p_right[1].wait_recv()
+    p_left[1].wait_recv()
+    first_quarter = last_weight(0)
+    last_mixed(0, acc)
+    last_add(0, first_quarter)
 
     @pl.when(core == 0)
     def _():
-        z_stage()
-
-    p_right[1].wait_recv()
-    p_left[1].wait_recv()
-    grow_mixed((z_left, 1), (z_right, 1), last=True)
+        z_stage(0, (0, 1))
+
+    p_right[2].wait_recv()
+    p_left[2].wait_recv()
+    last_mixed(1, e)
 
     @pl.loop(0, NH)
     def _(h):
@@ -507,9 +580,7 @@
 
     r_first = exchange(tx_r, rx_r, 2)
     rx_r[tm] = tx_r[tm]
-    grow_weight(z_left, 1)
-    grow_weight(z_right, 1)
-    add_pairs()
+    last_add(1, last_weight(1))
 
     def local_grads(h):
         for b in range(2):
@@ -538,6 +609,10 @@
     def _(h):
         local_grads(h)
 
+    @pl.when(core == 1)
+    def _():
+        z_stage(1, (0,))
+
     for copy in r_first:
         copy.wait_recv()
     part = jnp.zeros((32, DK), F32)
@@ -558,11 +633,16 @@
         local_grads(h)
 
     results[0].start()
+
     @pl.when(core == 1)
     def _():
-        z_stage()
-
-    y_arrivals(zl)
+        z_stage(1, (1,))
+        y_arrivals(zl, 1, (0, 1))
+
+    @pl.when(core == 0)
+    def _():
+        y_arrivals(zl, 0, (0,))
+
     for r in range(2):
         pair_own[r] = y_sum(zl, r)
     for copy in r_second:
@@ -585,7 +665,8 @@
 
     results[1].start()
     results[2].start()
-    z_copy.wait_recv()
+    for copy in z_copies:
+        copy.wait_recv()
     for r in range(2):
         rows = slice(r * HALF, (r + 1) * HALF)
         total = pair_own[r] + z_rx[rows, :].astype(F32)
@@ -683,18 +764,18 @@
             pltpu.VMEM((512, HALF), BF),
             dma((4,)),
             dma((6,)),
-            dma((18,)),
-            dma((18,)),
+            dma((22,)),
+            dma((22,)),
             dma((15,)),
             dma((15,)),
             dma((64,)),
             dma((64,)),
-            dma((16,)),
-            dma((16,)),
-            dma((16,)),
-            dma((2, 4, 2)),
-            dma((1,)),
-            dma((1,)),
+            dma((18,)),
+            dma((18,)),
+            dma((32,)),
+            dma((2, 4, 2, 2)),
+            dma((2,)),
+            dma((2,)),
         ],
         compiler_params=pltpu.CompilerParams(
             collective_id=0, has_side_effects=True, vmem_limit_bytes=66_000_000

time: 91.8 us -> 92.5 us (level)
  Pallas kernels: 90.2 us -> 91.5 us
    pallas_call x1, Pallas kernels: 86.9 us -> 88.3 us  [per_device(): pl.pallas_call(kernel, out_shape=shapes, in_specs=[pl.BlockSpec(memory_sp...]
where the time goes in v5:
time: 92.5 us; the launch traced here: 92.3 us
  Pallas kernels  91.5 us (99%)
    pallas_call x1, Pallas kernels, per_device(): pl.pallas_call(kernel, out_shape=shapes, in_specs=[pl.BlockSpec(memory_sp...  88.3 us
    pallas_call x1, Pallas kernels, per_device(): pl.pallas_call(hand_over, out_shape=shapes, in_specs=[anywhere] * 4, out_...  3.26 us

profile of v5, /device:TPU:1, one launch (start us, length us, event | category | flops | bytes accessed | tf_op | source)
XLA Modules:
  0.0 92.3 jit_solution(3214121120522194399)
XLA Ops:
  0.6 88.3 %shard_map.102 = (bf16[1024,512]{1,0:T(8,128)(2,1)}, bf16[1024,512]{1,0:T(8,128)(2,1)}, bf16[1024,512]{1,0:T(8,128)(2,1)}, f32[256,512]{1,0:T(8,128)}) custom-call(s32[4]{0:T(128)} %per_ref.1, f32[4,1024]{1,0:T(4,128)} %ld_ref.1, bf16[1024,512]{1,0:T(8,128)(2,1)} %q_hbm.1, bf16[1024,512]{1,0:T(8,128)(2,1)} %k_hbm.1, bf16[1024,512]{1,0:T(8,128)(2,1)} %v_hbm.1, ...), custom_call_target="tpu_custom_call" | custom-call | tf_op jit(solution)/shard_map/pallas_call | solution.py:723
  88.9 3.3 %shard_map.103 = (bf16[1024,512]{1,0:T(8,128)(2,1)}, bf16[1024,512]{1,0:T(8,128)(2,1)}, bf16[1024,512]{1,0:T(8,128)(2,1)}, f32[256,512]{1,0:T(8,128)}) custom-call(bf16[1024,512]{1,0:T(8,128)(2,1)} %get-tuple-element.8.refs_0_, bf16[1024,512]{1,0:T(8,128)(2,1)} %get-tuple-element.9.refs_1_, bf16[1024,512]{1,0:T(8,128)(2,1)} %get-tuple-element.10.refs_2_, ...), custom_call_target="tpu_custom_call" | custom-call | tf_op jit(solution)/shard_map/pallas_call | solution.py:784

commit v6 on v4

--- a/solution.py
+++ b/solution.py
@@ -321,6 +321,9 @@
     ]
     w_pair.append(w_copy(w_block(z_mate), z_mate, mate, 8))
 
+    pass_x(1)
+    pass_z(0)
+
     for copy in s_second:
         copy.wait_recv()
 
@@ -410,28 +413,26 @@
     loads[4].wait()
     grow_weight(hd, 0)
     grow_weight(hd, 1)
-    pass_x(1)
-    pass_z(0)
     add_pairs()
     for c in range(2):
         grow_weight(left, c)
         grow_weight(right, c)
+    add_pairs()
+    pass_far(0)
+    pass_z(1)
     for d in range(1, 4):
         src = tm_at(zl, lax.rem(y + 4 - d, 4), core)
         w_near[d - 1].wait_recv()
         w_pair.append(w_copy(w_block(src), src, mate, 8 + d))
-    add_pairs()
-    pass_far(0)
     grow_weight(across, 0)
     grow_weight(far, 0)
-    pass_z(1)
     add_pairs()
     grow_weight(across, 1)
+    pass_far(1)
     for d in range(1, 4):
         src = tm_at(1 - zl, lax.rem(y + 4 - d, 4), core)
         w_far[d - 1].wait_recv()
         w_pair.append(w_copy(w_block(src), src, mate, 11 + d))
-    pass_far(1)
     grow_weight(far, 1)
     add_pairs()
     loads[5].wait()
@@ -509,7 +510,6 @@
     rx_r[tm] = tx_r[tm]
     grow_weight(z_left, 1)
     grow_weight(z_right, 1)
-    add_pairs()
 
     def local_grads(h):
         for b in range(2):
@@ -534,7 +534,13 @@
             )
             dvp[b * BLK + HALF : (b + 1) * BLK, cols(h)] = mm_tn(wts[p, 2], eb[hi])
 
-    @pl.loop(0, 2)
+    @pl.loop(0, 1)
+    def _(h):
+        local_grads(h)
+
+    add_pairs()
+
+    @pl.loop(1, 2)
     def _(h):
         local_grads(h)
 

time: 91.8 us -> 92.3 us (level)
  no operation moved by 1% of the time
where the time goes in v6:
time: 92.3 us; the launch traced here: 91.7 us
  Pallas kernels  90.9 us (98%)
    pallas_call x1, Pallas kernels, per_device(): pl.pallas_call(kernel, out_shape=shapes, in_specs=[pl.BlockSpec(memory_sp...  87.7 us
    pallas_call x1, Pallas kernels, per_device(): pl.pallas_call(hand_over, out_shape=shapes, in_specs=[anywhere] * 4, out_...  3.26 us

profile of v6, /device:TPU:1, one launch (start us, length us, event | category | flops | bytes accessed | tf_op | source)
XLA Modules:
  0.0 91.7 jit_solution(2128255103952390843)
XLA Ops:
  0.6 87.7 %shard_map.102 = (bf16[1024,512]{1,0:T(8,128)(2,1)}, bf16[1024,512]{1,0:T(8,128)(2,1)}, bf16[1024,512]{1,0:T(8,128)(2,1)}, f32[256,512]{1,0:T(8,128)}) custom-call(s32[4]{0:T(128)} %per_ref.1, f32[4,1024]{1,0:T(4,128)} %ld_ref.1, bf16[1024,512]{1,0:T(8,128)(2,1)} %q_hbm.1, bf16[1024,512]{1,0:T(8,128)(2,1)} %k_hbm.1, bf16[1024,512]{1,0:T(8,128)(2,1)} %v_hbm.1, ...), custom_call_target="tpu_custom_call" | custom-call | tf_op jit(solution)/shard_map/pallas_call | solution.py:648
  88.3 3.3 %shard_map.103 = (bf16[1024,512]{1,0:T(8,128)(2,1)}, bf16[1024,512]{1,0:T(8,128)(2,1)}, bf16[1024,512]{1,0:T(8,128)(2,1)}, f32[256,512]{1,0:T(8,128)}) custom-call(bf16[1024,512]{1,0:T(8,128)(2,1)} %get-tuple-element.8.refs_0_, bf16[1024,512]{1,0:T(8,128)(2,1)} %get-tuple-element.9.refs_1_, bf16[1024,512]{1,0:T(8,128)(2,1)} %get-tuple-element.10.refs_2_, ...), custom_call_target="tpu_custom_call" | custom-call | tf_op jit(solution)/shard_map/pallas_call | solution.py:709
